TPU v7x, 128 devices: a whole 4x4x4 slice. The times are simulated.
128 devices in a mesh: scan: 4 (over x_lo, core), pix: 32 (over y, x_hi, z).
Axes of the slice: x: 4 (x_hi: 2, x_lo: 2; x = x_hi * 2 + x_lo), y: 4, z: 4, core: 2. Of those that a mesh axis runs over, the one named last changes fastest.
Arguments:
- raw_frames: float32 [6144, 128, 128], P(('scan', 'pix')), may hold values from 0.2 to 5
- gain_map: float32 [128, 128], replicated, may hold values from 0.5 to 1.5
- coupling: float32 [128, 128], replicated, may hold values from 0.05 to 0.25
- factor_w: float32 [6144, 256], P(('scan', 'pix')), may hold values from 0.01 to 0.25
- factor_h: float32 [256, 16384], P('scan', 'pix'), may hold values from 0.01 to 0.25
Outputs:
- w_factor: float32 [6144, 256], P(('scan', 'pix'))
- h_factor: float32 [256, 16384], P('scan', 'pix')
All inputs are finite; a program needn't handle non-finite values.
Results may differ from a plain program's by a relative error of at most 0.0003.
Values may be sent and summed in bfloat16 or wider, within the bound.
A program may use at most 64 MiB of HBM per device.

v0:
```python
import jax
import jax.numpy as jnp
from jax import lax
from jax.sharding import PartitionSpec as P

SWEEPS = 4
ITERS = 2


def correct(raw_frames, gain_map, coupling):
    measured = raw_frames * gain_map[None]
    couple_map = coupling[None]
    charge = measured
    for sweep in range(SWEEPS):
        padded = jnp.pad(charge, ((0, 0), (1, 1), (1, 1)))
        neighbours = (
            padded[:, 2:, 1:-1] + padded[:, :-2, 1:-1] + padded[:, 1:-1, 2:] + padded[:, 1:-1, :-2]
        )
        charge = (measured + couple_map * neighbours) / (1.0 + 4.0 * couple_map)
    return charge.reshape(raw_frames.shape[0], -1)


def local(raw_frames, gain_map, coupling, factor_w, factor_h):
    frame_rows = correct(raw_frames, gain_map, coupling)
    tile_data = lax.all_to_all(frame_rows, "pix", split_axis=1, concat_axis=0, tiled=True)
    comp_rows = factor_h.shape[0]
    w_local = factor_w
    h_local = factor_h
    w_round = lax.all_gather(factor_w.astype(jnp.bfloat16), "pix", axis=0, tiled=True)
    for rounds in range(ITERS):
        h_block = lax.all_gather(h_local.astype(jnp.bfloat16), "scan", axis=0, tiled=True)
        h_sums = lax.psum(jnp.sum(h_block.astype(jnp.float32), axis=1), "pix")
        product = jnp.dot(w_round, h_block, preferred_element_type=jnp.float32)
        count_ratio = (tile_data / product).astype(jnp.bfloat16)
        numerator = lax.psum_scatter(
            jnp.dot(count_ratio, h_block.T, preferred_element_type=jnp.float32),
            "pix",
            scatter_dimension=0,
            tiled=True,
        )
        w_local = w_local * numerator / h_sums
        w_round = lax.all_gather(w_local.astype(jnp.bfloat16), "pix", axis=0, tiled=True)
        local_sums = jnp.sum(w_local.astype(jnp.bfloat16).astype(jnp.float32), axis=0)
        w_sums = lax.psum(local_sums, ("scan", "pix"))
        product_two = jnp.dot(w_round, h_block, preferred_element_type=jnp.float32)
        ratio_two = (tile_data / product_two).astype(jnp.bfloat16)
        numerator_h = lax.psum_scatter(
            lax.dot_general(
                w_round, ratio_two, (((0,), (0,)), ((), ())), preferred_element_type=jnp.float32
            ),
            "scan",
            scatter_dimension=0,
            tiled=True,
        )
        own_sums = lax.dynamic_slice_in_dim(
            w_sums, lax.axis_index("scan") * comp_rows, comp_rows, 0
        )
        h_local = h_local * numerator_h / own_sums[:, None]
    return (w_local, h_local)


def solution(mesh):
    return jax.shard_map(
        local,
        mesh=mesh,
        in_specs=(
            P(("scan", "pix"), None, None),
            P(),
            P(),
            P(("scan", "pix"), None),
            P("scan", "pix"),
        ),
        out_specs=(P(("scan", "pix"), None), P("scan", "pix")),
        check_vma=False,
    )
```

profile of v0, /device:TPU:1, one launch (start us, length us, event | category | flops | bytes accessed | tf_op | source)
XLA Modules:
  0.0 956.6 jit_solution(9135922338065271615)
XLA Ops:
  8.0 2.1 broadcast_multiply_fusion
  10.2 1.9 fusion.5
  12.1 2.0 fusion.11
  14.1 2.0 fusion.17
  16.1 3.1 fusion.23
  19.2 2.9 all_to_all.14
  22.0 3.5 copy.8
  25.5 11.5 %all-to-all-start = ((f32[48,32,512]{2,0,1:T(8,128)}), f32[48,32,512]{2,0,1:T(8,128)S(1)}, u32[]{:S(2)}, u32[]{:S(2)}) async-start(f32[48,32,512]{2,0,1:T(8,128)} %copy.8), calls=%async_computation | async-start | bytes 6291456 | tf_op jit(solution)/shard_map/all_to_all | solution.py:25
  37.1 37.6 %all_gather.16 = bf16[256,512]{1,0:T(8,128)(2,1)S(1)} all-gather(bf16[64,512]{1,0:T(8,128)(2,1)S(1)} %convert_element_type.47), channel_id=1, replica_groups=mesh['scan'=4,'pix'=32] {'scan'}, dimensions={0}, use_global_device_ids=true | all-gather | bytes 327680 | tf_op jit(solution)/shard_map/all_gather | solution.py:31
  74.7 92.3 %all_gather.15 = bf16[1536,256]{1,0:T(8,128)(2,1)} all-gather(bf16[48,256]{1,0:T(8,128)(2,1)S(1)} %convert_element_type.46), channel_id=1, replica_groups=mesh['scan'=4,'pix'=32] {'pix'}, dimensions={0}, use_global_device_ids=true | all-gather | bytes 811008 | tf_op jit(solution)/shard_map/all_gather | solution.py:29
  167.0 1.7 fusion.24
  168.8 1.8 fusion.31
  170.7 75.6 %psum.28 = f32[256]{0:T(256)S(1)} all-reduce(f32[256]{0:T(256)S(1)} %convert_reduce_fusion.1), channel_id=1, replica_groups=mesh['scan'=4,'pix'=32] {'pix'}, use_global_device_ids=true, to_apply=%region_2.3 | all-reduce | flops 256 | bytes 2048 | tf_op jit(solution)/shard_map/psum | solution.py:32
  246.3 150.7 %reduce-scatter.5.cloned.1.call-done = f32[48,256]{1,0:T(8,128)} async-done(((f32[1536,256]{1,0:T(8,128)}), f32[48,256]{1,0:T(8,128)}) %reduce-scatter.5.cloned.1.call-update) | async-done | bytes 49168 | tf_op jit(solution)/shard_map/reduce_scatter | solution.py:35
  397.8 81.1 %all_gather.17 = bf16[1536,256]{1,0:T(8,128)(2,1)S(1)} all-gather(bf16[48,256]{1,0:T(8,128)(2,1)S(1)} %get-tuple-element.6), channel_id=1, replica_groups=mesh['scan'=4,'pix'=32] {'pix'}, dimensions={0}, use_global_device_ids=true | all-gather | bytes 811008 | tf_op jit(solution)/shard_map/all_gather | solution.py:42
  481.3 78.0 %psum.29 = f32[256]{0:T(256)S(1)} all-reduce(f32[256]{0:T(256)S(1)} %get-tuple-element.5), channel_id=1, replica_groups=mesh['scan'=4,'pix'=32] {'scan','pix'}, use_global_device_ids=true, to_apply=%region_5.6 | all-reduce | flops 256 | bytes 2048 | tf_op jit(solution)/shard_map/psum | solution.py:44
  560.4 6.6 all_gather.18
  566.9 1.7 fusion.26
  568.6 1.8 fusion.33
  570.6 77.5 %psum.30 = f32[256]{0:T(256)S(1)} all-reduce(f32[256]{0:T(256)S(1)} %convert_reduce_fusion), channel_id=1, replica_groups=mesh['scan'=4,'pix'=32] {'pix'}, use_global_device_ids=true, to_apply=%region_8.9 | all-reduce | flops 256 | bytes 2048 | tf_op jit(solution)/shard_map/psum | solution.py:32
  648.1 137.6 %reduce-scatter.9.cloned.1.call-done = f32[48,256]{1,0:T(8,128)} async-done(((f32[1536,256]{1,0:T(8,128)}), f32[48,256]{1,0:T(8,128)}) %reduce-scatter.9.cloned.1.call-update) | async-done | bytes 49168 | tf_op jit(solution)/shard_map/reduce_scatter | solution.py:35
  787.2 81.1 %all_gather.19 = bf16[1536,256]{1,0:T(8,128)(2,1)S(1)} all-gather(bf16[48,256]{1,0:T(8,128)(2,1)S(1)} %get-tuple-element.3), channel_id=1, replica_groups=mesh['scan'=4,'pix'=32] {'pix'}, dimensions={0}, use_global_device_ids=true | all-gather | bytes 811008 | tf_op jit(solution)/shard_map/all_gather | solution.py:42
  870.4 78.0 %psum.31 = f32[256]{0:T(256)S(1)} all-reduce(f32[256]{0:T(256)S(1)} %get-tuple-element.2), channel_id=1, replica_groups=mesh['scan'=4,'pix'=32] {'scan','pix'}, use_global_device_ids=true, to_apply=%region_11.12 | all-reduce | flops 256 | bytes 2048 | tf_op jit(solution)/shard_map/psum | solution.py:44
  948.4 1.7 multiply_divide_fusion
  (39 shorter events, 9.1 us)
Async XLA Ops:
  8.0 2.2 copy-start.2
  10.2 1.9 copy-start
  10.2 1.9 copy-start.4
  25.5 11.5 %copy-start.3 = (f32[64,512]{1,0:T(8,128)S(1)}, f32[64,512]{1,0:T(8,128)}, u32[]{:S(2)}) copy-start(f32[64,512]{1,0:T(8,128)} %param.9) | copy-start | bytes 393220
  25.5 11.6 %copy-start.6 = (f32[48,256]{1,0:T(8,128)S(1)}, f32[48,256]{1,0:T(8,128)}, u32[]{:S(2)}) copy-start(f32[48,256]{1,0:T(8,128)} %param.8) | copy-start | bytes 147460
  25.5 141.5 %all-to-all-start = ((f32[48,32,512]{2,0,1:T(8,128)}), f32[48,32,512]{2,0,1:T(8,128)S(1)}, u32[]{:S(2)}, u32[]{:S(2)}) async-start(f32[48,32,512]{2,0,1:T(8,128)} %copy.8), calls=%async_computation | async-start | bytes 6291456 | tf_op jit(solution)/shard_map/all_to_all | solution.py:25
  37.0 360.0 %reduce-scatter.5.cloned.1.call-start = ((), (), s32[]{:S(2)}) async-start(), calls=%async_computation.5 | async-start | bytes 1622016 | tf_op jit(solution)/shard_map/reduce_scatter | solution.py:35
  170.5 388.8 %reduce-scatter.7.cloned.1.call-start = ((), (), s32[]{:S(2)}) async-start(), calls=%async_computation.6 | async-start | bytes 655360 | tf_op jit(solution)/shard_map/reduce_scatter | solution.py:47
  478.9 0.9 copy-start.1
  481.2 304.5 %reduce-scatter.9.cloned.1.call-start = ((), (), s32[]{:S(2)}) async-start(), calls=%async_computation.7 | async-start | bytes 1622016 | tf_op jit(solution)/shard_map/reduce_scatter | solution.py:35
  570.4 378.0 %reduce-scatter.11.cloned.1.call-start = ((), (), s32[]{:S(2)}) async-start(), calls=%async_computation.8 | async-start | bytes 655360 | tf_op jit(solution)/shard_map/reduce_scatter | solution.py:47
  868.9 79.5 %copy-start.5 = (f32[64,512]{1,0:T(8,128)S(1)}, f32[64,512]{1,0:T(8,128)}, u32[]{:S(2)}) copy-start(f32[64,512]{1,0:T(8,128)} %reduce-scatter.7.cloned.1.call-done) | copy-start | bytes 393220
Sparse Core Ops, SparseCore 0:
  170.7 226.2 reduce-scatter.4
  481.3 28.4 reduce-scatter.6
  570.5 215.1 reduce-scatter.8
  870.5 28.2 reduce-scatter.10
where the time goes:
time: 957 us
  blocking collectives  608 us (64%)
  waiting for transfers between devices  288 us (30%)
  other arithmetic  17.1 us (2%)
  between operations  13.9 us (1%)
  starting transfers between devices  11.6 us (1%)
  matrix products  10.9 us (1%)
    reduce_scatter x2, waiting for transfers between devices, local(): lax.psum_scatter(jnp.dot(count_ratio, h_block.T, preferred_element_type=j...  288 us
    all_gather x2, blocking collectives, local(): lax.all_gather(w_local.astype(jnp.bfloat16), 'pix', axis=0, tiled=True)  162 us
    psum x2, blocking collectives, local(): w_sums = lax.psum(local_sums, ('scan', 'pix'))  156 us
    psum x2, blocking collectives, local(): h_sums = lax.psum(jnp.sum(h_block.astype(jnp.float32), axis=1), 'pix')  153 us
    all_gather x1, blocking collectives, local(): lax.all_gather(factor_w.astype(jnp.bfloat16), 'pix', axis=0, tiled=True)  92.3 us
    all_gather x2, blocking collectives, local(): lax.all_gather(h_local.astype(jnp.bfloat16), 'scan', axis=0, tiled=True)  44.2 us
  transfers between devices with their start and end apart: 5, of which 2 were waited for; matrix products, arithmetic and copies ran while one was open for 0% of the time, Pallas kernels for 0%

commit v1 on v0

v1 whole, which is shorter than its diff:
```python
import functools

import jax
import jax.numpy as jnp
from jax import lax
from jax.experimental import pallas as pl
from jax.experimental.pallas import tpu as pltpu
from jax.sharding import PartitionSpec as P

SWEEPS = 4
ITERS = 2
FRAME = 128
LANES = 128
EXTENTS = (4, 2, 4)
GROUP = 16
DATA = jnp.float32
SUMS = 8
CHUNK = 4

MESH = pl.DeviceIdType.MESH
F32 = jnp.float32
BF16 = jnp.bfloat16


def kernel(
    n_scan,
    n_pix,
    raw_ref,
    gain_ref,
    couple_ref,
    w_ref,
    h_ref,
    w_out,
    h_out,
    raw_v,
    maps,
    charge,
    tile,
    w_all,
    w_now,
    num_send,
    num_recv,
    h_all,
    h_now,
    ratio,
    numh_send,
    numh_recv,
    raw_sem,
    data_sems,
    own_sem,
    w_sems,
    num_sems,
    h_sems,
    numh_sems,
):
    rows = w_ref.shape[0]
    rank = w_ref.shape[1]
    comps = h_ref.shape[0]
    pixels = h_ref.shape[1]
    block = FRAME // n_pix
    groups = rows // GROUP
    scan = lax.axis_index("scan")
    pix = lax.axis_index("pix")
    ey, ex, ez = EXTENTS
    my, mx, mz = pix // (ex * ez), (pix // ez) % ex, pix % ez

    def ahead(slot):
        dy, dx, dz = slot // (ex * ez), (slot // ez) % ex, slot % ez
        return (((my + dy) % ey) * ex + (mx + dx) % ex) * ez + (mz + dz) % ez

    def behind(slot):
        dy, dx, dz = slot // (ex * ez), (slot // ez) % ex, slot % ez
        return (((my + ey - dy) % ey) * ex + (mx + ex - dx) % ex) * ez + (mz + ez - dz) % ez

    def remote(src, dst, sems, to_scan, to_pix):
        return pltpu.make_async_remote_copy(
            src_ref=src,
            dst_ref=dst,
            send_sem=sems.at[0],
            recv_sem=sems.at[1],
            device_id=(to_scan, to_pix),
            device_id_type=MESH,
        )

    def drain(ref, sem):
        pltpu.make_async_copy(ref, ref, sem).wait()

    for g in range(groups):
        pltpu.make_async_copy(
            raw_ref.at[pl.ds(g * GROUP * FRAME, GROUP * FRAME)], raw_v.at[g], raw_sem.at[g]
        ).start()

    barrier = pltpu.get_barrier_semaphore()

    def greet(slot, carry):
        pl.semaphore_signal(
            barrier, inc=1, device_id=(scan, ahead(slot)), device_id_type=MESH
        )
        return carry

    lax.fori_loop(1, n_pix, greet, 0)
    for j in range(1, n_scan):
        pl.semaphore_signal(
            barrier, inc=1, device_id=((scan + j) % n_scan, pix), device_id_type=MESH
        )

    pad = maps.shape[1] - FRAME
    coupling = couple_ref[...]
    inverse = 1.0 / (1.0 + 4.0 * coupling)
    gain = gain_ref[...]
    zero_rows = jnp.zeros((pad // 2, LANES), F32)
    for i, value in enumerate((gain, gain * inverse, coupling * inverse)):
        maps[i, pl.ds(0, pad // 2), :] = zero_rows
        maps[i, pl.ds(pad // 2, FRAME), :] = value
        maps[i, pl.ds(pad // 2 + FRAME, pad // 2), :] = zero_rows

    w_now[...] = w_ref[...]
    h_now[...] = h_ref[...]
    w_all[0, 0] = w_ref[...].astype(BF16)
    my_rows = pl.ds(pl.multiple_of(scan * comps, comps), comps)
    h_all[0, my_rows, :] = h_ref[...].astype(BF16)

    pl.semaphore_wait(barrier, n_pix - 1 + n_scan - 1)

    def send_w(step):
        def go(slot, carry):
            remote(
                w_all.at[step, 0], w_all.at[step, slot], w_sems.at[step], scan, ahead(slot)
            ).start()
            return carry

        lax.fori_loop(1, n_pix, go, 0)

    def send_h(step):
        for j in range(1, n_scan):
            remote(
                h_all.at[step, my_rows],
                h_all.at[step, my_rows],
                h_sems.at[step],
                (scan + j) % n_scan,
                pix,
            ).start()

    def wait_w(step, which):
        drain(w_all.at[step, pl.ds(1, n_pix - 1)], w_sems.at[step, which])

    def wait_h(step, which):
        drain(h_all.at[step, pl.ds(0, comps * (n_scan - 1))], h_sems.at[step, which])

    send_h(0)
    send_w(0)

    lane = lax.broadcasted_iota(jnp.int32, (GROUP, LANES), 1)
    first, last = lane == 0, lane == LANES - 1
    half = pad // 2

    def correct(g):
        def map_row(i, r):
            return jnp.broadcast_to(maps[i, pl.ds(r, 1), :], (GROUP, LANES))

        def step(t, carry):
            older, mids, scaled = carry
            raw = raw_v[g, pl.ds(t % FRAME, GROUP, stride=FRAME), :]
            fresh = raw * map_row(0, t + half)
            new_older, new_mids = [], []
            new_scaled = [raw * map_row(1, t + half)] + list(scaled[:-1])
            for s in range(SWEEPS):
                up, mid = older[s], mids[s]
                left = jnp.where(first, 0.0, pltpu.roll(mid, 1, 1))
                right = jnp.where(last, 0.0, pltpu.roll(mid, LANES - 1, 1))
                new_older.append(mid)
                new_mids.append(fresh)
                fresh = scaled[s] + map_row(2, t + half - 1 - s) * (
                    (up + fresh) + (left + right)
                )
            charge[t, pl.ds(g * GROUP, GROUP), :] = fresh.astype(charge.dtype)
            return tuple(new_older), tuple(new_mids), tuple(new_scaled)

        zero = maps[0, pl.ds(0, GROUP), :]
        zeros = (zero,) * SWEEPS
        lax.fori_loop(0, FRAME + SWEEPS, step, (zeros, zeros, zeros))

    def block_of(device):
        return pl.ds(SWEEPS + device * block, block)

    for g in range(groups):
        pltpu.make_async_copy(
            raw_ref.at[pl.ds(g * GROUP * FRAME, GROUP * FRAME)], raw_v.at[g], raw_sem.at[g]
        ).wait()
        correct(g)
        frames = pl.ds(g * GROUP, GROUP)
        pltpu.make_async_copy(
            charge.at[block_of(pix), frames], tile.at[0, :, frames], own_sem.at[g]
        ).start()

        def go(slot, carry):
            to = ahead(slot)
            remote(
                charge.at[block_of(to), frames],
                tile.at[slot, :, frames],
                data_sems.at[g],
                scan,
                to,
            ).start()
            return carry

        lax.fori_loop(1, n_pix, go, 0)

    wait_h(0, 1)
    wait_w(0, 1)
    for g in range(groups):
        frames = pl.ds(g * GROUP, GROUP)
        pltpu.make_async_copy(
            charge.at[block_of(pix), frames], tile.at[0, :, frames], own_sem.at[g]
        ).wait()
        drain(tile.at[pl.ds(1, n_pix - 1), :, frames], data_sems.at[g, 1])

    steps = n_pix // CHUNK
    size = CHUNK * rows

    def ratios(step_w, step_h, c):
        slots = pl.ds(c * CHUNK, CHUNK)
        w = w_all[step_w, slots].reshape(size, rank)
        product = jnp.dot(w, h_all[step_h], preferred_element_type=F32)
        parts = []
        for k in range(block):
            data = tile[slots, k].reshape(size, LANES).astype(F32)
            parts.append((data / product[:, k * LANES : (k + 1) * LANES]).astype(BF16))
        return w, jnp.concatenate(parts, axis=1)

    for it in range(ITERS):
        if it > 0:
            wait_h(it, 1)
            drain(num_send.at[pl.ds(1, n_pix - 1)], num_sems.at[it - 1, 0])
        sums = lax.dot_general(
            jnp.ones((SUMS, pixels), BF16),
            h_all[it],
            (((1,), (1,)), ((), ())),
            preferred_element_type=F32,
        )

        def numerators(c, carry, skip=0):
            _, count_ratio = ratios(it, it, c)
            part = lax.dot_general(
                count_ratio, h_all[it], (((1,), (1,)), ((), ())), preferred_element_type=F32
            )
            slots = pl.ds(c * CHUNK, CHUNK)
            num_send[slots, pl.ds(0, rows), :] = part.reshape(CHUNK, rows, rank)
            num_send[slots, pl.ds(rows, SUMS), :] = jnp.broadcast_to(
                sums[None], (CHUNK, SUMS, rank)
            )

            def go(slot, carry):
                remote(
                    num_send.at[slot], num_recv.at[it, slot], num_sems.at[it], scan, behind(slot)
                ).start()
                return carry

            return lax.fori_loop(c * CHUNK + skip, (c + 1) * CHUNK, go, carry)

        numerators(0, 0, skip=1)
        lax.fori_loop(1, steps, numerators, 0)
        drain(num_recv.at[it, pl.ds(1, n_pix - 1)], num_sems.at[it, 1])

        def add(slot, total):
            return total + num_recv[it, slot]

        total = lax.fori_loop(1, n_pix, add, num_send[0])
        w_new = w_now[...] * total[:rows] / total[rows : rows + 1]
        if it == ITERS - 1:
            w_out[...] = w_new
        w_now[...] = w_new
        w_all[it + 1, 0] = w_new.astype(BF16)
        send_w(it + 1)
        wait_w(it + 1, 1)

        def second(c, carry):
            _, count_ratio = ratios(it + 1, it, c)
            ratio[pl.ds(c * size, size), pl.ds(0, pixels)] = count_ratio
            return carry

        ratio[:, pl.ds(pixels, LANES)] = jnp.ones((n_pix * rows, LANES), BF16)
        lax.fori_loop(0, steps, second, 0)
        if it > 0:
            drain(numh_send.at[pl.ds(0, comps * (n_scan - 1))], numh_sems.at[it - 1, 0])
        numh_send[...] = lax.dot_general(
            w_all[it + 1].reshape(n_pix * rows, rank),
            ratio[...],
            (((0,), (0,)), ((), ())),
            preferred_element_type=F32,
        )
        for j in range(1, n_scan):
            to = (scan + j) % n_scan
            remote(
                numh_send.at[pl.ds(pl.multiple_of(to * comps, comps), comps)],
                numh_recv.at[it, j - 1],
                numh_sems.at[it],
                to,
                pix,
            ).start()
        drain(numh_recv.at[it], numh_sems.at[it, 1])
        total_h = numh_send[my_rows, :]
        for j in range(n_scan - 1):
            total_h = total_h + numh_recv[it, j]
        w_sum = total_h[:, pixels:]
        for k in range(block):
            columns = slice(k * LANES, (k + 1) * LANES)
            h_new = h_now[:, columns] * total_h[:, columns] / w_sum
            h_now[:, columns] = h_new
            if it == ITERS - 1:
                h_out[:, columns] = h_new
        if it < ITERS - 1:
            h_all[it + 1, my_rows, :] = h_now[...].astype(BF16)
            send_h(it + 1)

    for g in range(groups):
        frames = pl.ds(g * GROUP, GROUP)
        drain(tile.at[pl.ds(1, n_pix - 1), :, frames], data_sems.at[g, 0])
    for step in range(ITERS + 1):
        wait_w(step, 0)
    for step in range(ITERS):
        wait_h(step, 0)
    drain(num_send.at[pl.ds(1, n_pix - 1)], num_sems.at[ITERS - 1, 0])
    drain(numh_send.at[pl.ds(0, comps * (n_scan - 1))], numh_sems.at[ITERS - 1, 0])


def solution(mesh):
    n_scan, n_pix = mesh.shape["scan"], mesh.shape["pix"]

    def local(raw_frames, gain_map, coupling, factor_w, factor_h):
        frames = raw_frames.shape[0]
        rank = factor_w.shape[1]
        comps, pixels = factor_h.shape
        groups = frames // GROUP
        block = FRAME // n_pix
        vmem = pl.BlockSpec(memory_space=pltpu.VMEM)
        dma = pltpu.SemaphoreType.DMA
        return pl.pallas_call(
            functools.partial(kernel, n_scan, n_pix),
            out_shape=(
                jax.ShapeDtypeStruct(factor_w.shape, F32),
                jax.ShapeDtypeStruct(factor_h.shape, F32),
            ),
            in_specs=[pl.BlockSpec(memory_space=pl.ANY)] + [vmem] * 4,
            out_specs=(vmem, vmem),
            scratch_shapes=[
                pltpu.VMEM((groups, GROUP * FRAME, LANES), F32),
                pltpu.VMEM((3, FRAME + 2 * GROUP, LANES), F32),
                pltpu.VMEM((FRAME + SWEEPS, frames, LANES), DATA),
                pltpu.VMEM((n_pix, block, frames, LANES), DATA),
                pltpu.VMEM((ITERS + 1, n_pix, frames, rank), BF16),
                pltpu.VMEM((frames, rank), F32),
                pltpu.VMEM((n_pix, frames + SUMS, rank), F32),
                pltpu.VMEM((ITERS, n_pix, frames + SUMS, rank), F32),
                pltpu.VMEM((ITERS, rank, pixels), BF16),
                pltpu.VMEM((comps, pixels), F32),
                pltpu.VMEM((n_pix * frames, pixels + LANES), BF16),
                pltpu.VMEM((rank, pixels + LANES), F32),
                pltpu.VMEM((ITERS, n_scan - 1, comps, pixels + LANES), F32),
                dma((groups,)),
                dma((groups, 2)),
                dma((groups,)),
                dma((ITERS + 1, 2)),
                dma((ITERS, 2)),
                dma((ITERS, 2)),
                dma((ITERS, 2)),
            ],
            compiler_params=pltpu.CompilerParams(
                collective_id=0, has_side_effects=True, vmem_limit_bytes=58 * 1024 * 1024
            ),
        )(raw_frames.reshape(frames * FRAME, LANES), gain_map, coupling, factor_w, factor_h)

    return jax.shard_map(
        local,
        mesh=mesh,
        in_specs=(
            P(("scan", "pix"), None, None),
            P(),
            P(),
            P(("scan", "pix"), None),
            P("scan", "pix"),
        ),
        out_specs=(P(("scan", "pix"), None), P("scan", "pix")),
        check_vma=False,
    )
```

time: 957 us -> 172 us (0.18)
  blocking collectives: 608 us -> 0 us
  waiting for transfers between devices: 288 us -> 0 us
  Pallas kernels: 0 us -> 168 us
  other arithmetic: 17.1 us -> 0 us
  between operations: 13.9 us -> 0.64 us
  starting transfers between devices: 11.6 us -> 0 us
  matrix products: 10.9 us -> 0 us
    psum x4 -> x0, blocking collectives: 309 us -> none  [the longest x2 156 us: local(): w_sums = lax.psum(local_sums, ('scan', 'pix'))]
    all_gather x5 -> x0, blocking collectives: 299 us -> none  [the longest x2 162 us: local(): lax.all_gather(w_local.astype(jnp.bfloat16), 'pix', axis=0, tiled=True)]
    reduce_scatter x4 -> x0, waiting for transfers between devices: 288 us -> none  [the longest x2 288 us: local(): lax.psum_scatter(jnp.dot(count_ratio, h_block.T, preferred_element_type=j...]
    pallas_call x0 -> x1, Pallas kernels: none -> 168 us  [local(): pl.pallas_call(functools.partial(kernel, n_scan, n_pix), out_shape=(jax.S...]
    all_to_all x1 -> x0, starting transfers between devices: 11.5 us -> none  [local(): lax.all_to_all(frame_rows, 'pix', split_axis=1, concat_axis=0, tiled=True)]
    dot_general x8 -> x0, matrix products: 10.9 us -> none  [the longest x2 3.51 us: local(): jnp.dot(count_ratio, h_block.T, preferred_element_type=jnp.float32)]
    div x5 -> x0, other arithmetic: 10.6 us -> none  [the longest x4 8.92 us: correct(): charge = (measured + couple_map * neighbours) / (1.0 + 4.0 * couple_map)]
  transfers between devices with their start and end apart: 5 -> 0, of which waited for: 2 -> 0; matrix products, arithmetic and copies ran while one was open for 0% -> 0% of each run, Pallas kernels for 0% -> 0%
where the time goes in v1:
time: 172 us; the launch traced here: 171 us
  Pallas kernels  168 us (98%)
  local copies, waits for them, and re-layouts  2.99 us (2%)
    pallas_call x1, Pallas kernels, local(): pl.pallas_call(functools.partial(kernel, n_scan, n_pix), out_shape=(jax.S...  168 us

profile of v1, /device:TPU:1, one launch (start us, length us, event | category | flops | bytes accessed | tf_op | source)
XLA Modules:
  0.0 171.4 jit_solution(2399183030656987961)
XLA Ops:
  0.6 167.8 %shard_map.68 = (f32[48,256]{1,0:T(8,128)}, f32[64,512]{1,0:T(8,128)}) custom-call(f32[6144,128]{1,0:T(8,128)} %bitcast.1, f32[128,128]{1,0:T(8,128)} %gain_ref.1, f32[128,128]{1,0:T(8,128)} %couple_ref.1, f32[48,256]{1,0:T(8,128)} %w_ref.1, f32[64,512]{1,0:T(8,128)} %h_ref.1), custom_call_target="tpu_custom_call" | custom-call | tf_op jit(solution)/shard_map/pallas_call | solution.py:338
  168.4 1.4 copy.9
  169.8 1.6 copy.10

commit v2 on v1

v2 whole, which is shorter than its diff:
```python
import functools

import jax
import jax.numpy as jnp
from jax import lax
from jax.experimental import pallas as pl
from jax.experimental.pallas import tpu as pltpu
from jax.sharding import PartitionSpec as P

SWEEPS = 4
ITERS = 2
FRAME = 128
LANES = 128
EY, EX, EZ = 4, 2, 4
SLOTS = EY * EZ
GROUP = 16
ROWS = 64
DATA = jnp.bfloat16
CHUNK = 4

MESH = pl.DeviceIdType.MESH
F32 = jnp.float32
BF16 = jnp.bfloat16


def kernel(
    n_scan,
    raw_ref,
    gain_ref,
    couple_ref,
    w_ref,
    h_ref,
    w_out,
    h_out,
    raw_v,
    maps,
    scaled,
    field,
    charge,
    tile,
    w_all,
    w_now,
    num_send,
    num_recv,
    h_all,
    h_now,
    hsum_all,
    ratio,
    numh_send,
    numh_recv,
    wsum_all,
    raw_sem,
    data_sems,
    own_sem,
    w_sems,
    num_sems,
    h_sems,
    hsum_sems,
    numh_sems,
    wsum_sems,
):
    rows, rank = w_ref.shape
    comps, pixels = h_ref.shape
    block = pixels // FRAME
    groups = rows // GROUP
    mates = EX * n_scan
    scan = lax.axis_index("scan")
    pix = lax.axis_index("pix")
    my, mx, mz = pix // (EX * EZ), (pix // EZ) % EX, pix % EZ

    def ahead(slot):
        return (my + slot // EZ) % EY, (mz + slot % EZ) % EZ

    def behind(slot):
        return (my + EY - slot // EZ) % EY, (mz + EZ - slot % EZ) % EZ

    def mate(j):
        other = (mx * n_scan + scan + j) % mates
        return other % n_scan, other // n_scan

    def remote(src, dst, sems, to_scan, y, x, z):
        return pltpu.make_async_remote_copy(
            src_ref=src,
            dst_ref=dst,
            send_sem=sems.at[0],
            recv_sem=sems.at[1],
            device_id=(to_scan, (y * EX + x) * EZ + z),
            device_id_type=MESH,
        )

    def to_slot(src, dst, sems, where):
        y, z = where
        return remote(src, dst, sems, scan, y, mx, z)

    def to_mate(src, dst, sems, j):
        to_scan, x = mate(j)
        return remote(src, dst, sems, to_scan, my, x, mz)

    def drain(ref, sem):
        pltpu.make_async_copy(ref, ref, sem).wait()

    def fetch(g):
        return pltpu.make_async_copy(
            raw_ref.at[pl.ds(g * GROUP * FRAME, GROUP * FRAME)], raw_v.at[g], raw_sem.at[g]
        )

    for g in range(groups):
        fetch(g).start()

    barrier = pltpu.get_barrier_semaphore()

    def greet(slot, carry):
        y, z = ahead(slot)
        pl.semaphore_signal(
            barrier, inc=1, device_id=(scan, (y * EX + mx) * EZ + z), device_id_type=MESH
        )
        return carry

    lax.fori_loop(1, SLOTS, greet, 0)
    for j in range(1, mates):
        to_scan, x = mate(j)
        pl.semaphore_signal(
            barrier, inc=1, device_id=(to_scan, (my * EX + x) * EZ + mz), device_id_type=MESH
        )

    coupling = couple_ref[...]
    inverse = 1.0 / (1.0 + 4.0 * coupling)
    gain = gain_ref[...]
    for i, value in enumerate((gain, gain * inverse, coupling * inverse)):
        maps[i] = jnp.broadcast_to(value[:, None, :], (FRAME, 8, LANES))

    w_now[...] = w_ref[...]
    h_now[...] = h_ref[...]
    w_all[0, 0] = w_ref[...].astype(BF16)
    my_comps = pl.ds(pl.multiple_of(scan * comps, comps), comps)
    my_pixels = pl.ds(pl.multiple_of(mx * pixels, pixels), pixels)
    h_all[0, my_comps, my_pixels] = h_ref[...].astype(BF16)

    pl.semaphore_wait(barrier, SLOTS - 1 + mates - 1)

    def send_w(step):
        def go(slot, carry):
            to_slot(
                w_all.at[step, 0], w_all.at[step, slot], w_sems.at[step], ahead(slot)
            ).start()
            return carry

        lax.fori_loop(1, SLOTS, go, 0)

    def send_h(step):
        own = h_all.at[step, my_comps, my_pixels]
        for j in range(1, mates):
            to_mate(own, own, h_sems.at[step], j).start()

    def wait_w(step, which):
        drain(w_all.at[step, pl.ds(1, SLOTS - 1)], w_sems.at[step, which])

    def wait_h(step, which):
        drain(
            h_all.at[step, pl.ds(0, rank * (mates - 1) // mates)], h_sems.at[step, which]
        )

    send_h(0)
    send_w(0)

    lane = lax.broadcasted_iota(jnp.int32, (ROWS, GROUP, LANES), 2)
    first, last = lane == 0, lane == LANES - 1

    for i in range(2):
        edge = jnp.zeros((GROUP, LANES), F32)
        field[i, 0] = edge
        field[i, FRAME + 1] = edge

    def correct(g):
        def map_rows(i, at):
            value = maps[i, pl.ds(at, ROWS)]
            return jnp.concatenate([value] * (GROUP // 8), axis=1)

        def start(c, carry):
            at = c * 8
            for i in range(8):
                raw = raw_v[g, pl.ds(at + i, GROUP, stride=FRAME), :]
                tall = [maps[m, at + i] for m in range(2)]
                gain_row, scaled_row = [
                    jnp.concatenate([v] * (GROUP // 8), axis=0) for v in tall
                ]
                field[0, at + i + 1] = raw * gain_row
                scaled[at + i] = raw * scaled_row
            return carry

        lax.fori_loop(0, FRAME // 8, start, 0)
        for s in range(SWEEPS):

            def sweep(c, carry):
                at = c * ROWS
                rows_in = field[s % 2, pl.ds(at, ROWS + 2)]
                mid = rows_in[1:-1]
                left = jnp.where(first, 0.0, pltpu.roll(mid, 1, 2))
                right = jnp.where(last, 0.0, pltpu.roll(mid, LANES - 1, 2))
                value = scaled[pl.ds(at, ROWS)] + map_rows(2, at) * (
                    (rows_in[:-2] + rows_in[2:]) + (left + right)
                )
                if s == SWEEPS - 1:
                    slabs = ROWS // (EX * EZ * block)
                    charge[pl.ds(c * slabs, slabs), :, :, :, pl.ds(g * GROUP, GROUP), :] = (
                        value.astype(charge.dtype).reshape(slabs, EX, EZ, block, GROUP, LANES)
                    )
                else:
                    field[(s + 1) % 2, pl.ds(at + 1, ROWS)] = value
                return carry

            lax.fori_loop(0, FRAME // ROWS, sweep, 0)

    def own_copy(g):
        frames = pl.ds(g * GROUP, GROUP)
        return pltpu.make_async_copy(
            charge.at[my, :, mz, :, frames], tile.at[0, :, :, frames], own_sem.at[g]
        )

    for g in range(groups):
        fetch(g).wait()
        correct(g)
        own_copy(g).start()
        frames = pl.ds(g * GROUP, GROUP)

        def go(slot, carry):
            y, z = ahead(slot)
            to_slot(
                charge.at[y, :, z, :, frames],
                tile.at[slot, :, :, frames],
                data_sems.at[g],
                (y, z),
            ).start()
            return carry

        lax.fori_loop(1, SLOTS, go, 0)

    steps = SLOTS // CHUNK
    size = CHUNK * rows
    wide = EX * pixels

    def ratios(step_w, step_h, c):
        slots = pl.ds(c * CHUNK, CHUNK)
        w = w_all[step_w, slots].reshape(size, rank)
        product = jnp.dot(w, h_all[step_h], preferred_element_type=F32)
        parts = []
        for x in range(EX):
            for k in range(block):
                at = (x * block + k) * LANES
                data = tile[slots, x, k].reshape(size, LANES).astype(F32)
                parts.append((data / product[:, at : at + LANES]).astype(BF16))
        return jnp.concatenate(parts, axis=1)

    def column_sums(lhs_rows, operand, dims):
        ones = jnp.ones((8, lhs_rows), BF16)
        return lax.dot_general(ones, operand, (dims, ((), ())), preferred_element_type=F32)[:1]

    for it in range(ITERS):
        wait_h(it, 1)
        hsum_all[it, 0] = column_sums(wide, h_all[it], ((1,), (1,)))

        def share(slot, carry):
            to_slot(
                hsum_all.at[it, 0], hsum_all.at[it, slot], hsum_sems.at[it], ahead(slot)
            ).start()
            return carry

        lax.fori_loop(1, SLOTS, share, 0)
        if it == 0:
            wait_w(0, 1)
            for g in range(groups):
                frames = pl.ds(g * GROUP, GROUP)
                own_copy(g).wait()
                drain(tile.at[pl.ds(1, SLOTS - 1), :, :, frames], data_sems.at[g, 1])
        else:
            drain(num_send.at[pl.ds(1, SLOTS - 1)], num_sems.at[it - 1, 0])

        def numerators(c, carry, skip=0):
            part = lax.dot_general(
                ratios(it, it, c),
                h_all[it],
                (((1,), (1,)), ((), ())),
                preferred_element_type=F32,
            )
            num_send[pl.ds(c * CHUNK, CHUNK)] = part.reshape(CHUNK, rows, rank)

            def go(slot, carry):
                to_slot(
                    num_send.at[slot], num_recv.at[it, slot], num_sems.at[it], behind(slot)
                ).start()
                return carry

            return lax.fori_loop(c * CHUNK + skip, (c + 1) * CHUNK, go, carry)

        numerators(0, 0, skip=1)
        lax.fori_loop(1, steps, numerators, 0)
        drain(hsum_all.at[it, pl.ds(1, SLOTS - 1)], hsum_sems.at[it, 1])
        h_sum = hsum_all[it, 0]
        for slot in range(1, SLOTS):
            h_sum = h_sum + hsum_all[it, slot]
        drain(num_recv.at[it, pl.ds(1, SLOTS - 1)], num_sems.at[it, 1])

        def add(slot, total):
            return total + num_recv[it, slot]

        total = lax.fori_loop(1, SLOTS, add, num_send[0])
        w_new = w_now[...] * total / h_sum
        if it == ITERS - 1:
            w_out[...] = w_new
        w_now[...] = w_new
        w_all[it + 1, 0] = w_new.astype(BF16)
        send_w(it + 1)
        wait_w(it + 1, 1)
        wsum_all[it, 0] = column_sums(
            SLOTS * rows, w_all[it + 1].reshape(SLOTS * rows, rank), ((1,), (0,))
        )
        for j in range(1, mates):
            to_mate(wsum_all.at[it, 0], wsum_all.at[it, j], wsum_sems.at[it], j).start()

        def second(c, carry):
            ratio[pl.ds(c * size, size), :] = ratios(it + 1, it, c)
            return carry

        lax.fori_loop(0, steps, second, 0)
        if it > 0:
            drain(numh_send.at[pl.ds(1, mates - 1)], numh_sems.at[it - 1, 0])
        for x in range(EX):
            numh_send[pl.ds(x * n_scan, n_scan)] = lax.dot_general(
                w_all[it + 1].reshape(SLOTS * rows, rank),
                ratio[:, x * pixels : (x + 1) * pixels],
                (((0,), (0,)), ((), ())),
                preferred_element_type=F32,
            ).reshape(n_scan, comps, pixels)
        for j in range(1, mates):
            to_scan, x = mate(j)
            to_mate(
                numh_send.at[x * n_scan + to_scan], numh_recv.at[it, j - 1], numh_sems.at[it], j
            ).start()
        drain(wsum_all.at[it, pl.ds(1, mates - 1)], wsum_sems.at[it, 1])
        w_sum = wsum_all[it, 0]
        for j in range(1, mates):
            w_sum = w_sum + wsum_all[it, j]
        at = lax.broadcasted_iota(jnp.int32, (comps, rank), 1)
        own = lax.broadcasted_iota(jnp.int32, (comps, rank), 0) + scan * comps
        w_sum = jnp.sum(
            jnp.where(at == own, jnp.broadcast_to(w_sum, (comps, rank)), 0.0),
            axis=1,
            keepdims=True,
        )
        drain(numh_recv.at[it], numh_sems.at[it, 1])
        total_h = numh_send[mx * n_scan + scan]
        for j in range(mates - 1):
            total_h = total_h + numh_recv[it, j]
        h_new = h_now[...] * total_h / w_sum
        if it == ITERS - 1:
            h_out[...] = h_new
        else:
            h_now[...] = h_new
            h_all[it + 1, my_comps, my_pixels] = h_new.astype(BF16)
            send_h(it + 1)

    for g in range(groups):
        frames = pl.ds(g * GROUP, GROUP)
        drain(tile.at[pl.ds(1, SLOTS - 1), :, :, frames], data_sems.at[g, 0])
    for step in range(ITERS + 1):
        wait_w(step, 0)
    for step in range(ITERS):
        wait_h(step, 0)
        drain(hsum_all.at[step, pl.ds(1, SLOTS - 1)], hsum_sems.at[step, 0])
        drain(wsum_all.at[step, pl.ds(1, mates - 1)], wsum_sems.at[step, 0])
    drain(num_send.at[pl.ds(1, SLOTS - 1)], num_sems.at[ITERS - 1, 0])
    drain(numh_send.at[pl.ds(1, mates - 1)], numh_sems.at[ITERS - 1, 0])


def solution(mesh):
    n_scan = mesh.shape["scan"]
    mates = EX * n_scan

    def local(raw_frames, gain_map, coupling, factor_w, factor_h):
        frames = raw_frames.shape[0]
        rank = factor_w.shape[1]
        comps, pixels = factor_h.shape
        groups = frames // GROUP
        block = pixels // FRAME
        vmem = pl.BlockSpec(memory_space=pltpu.VMEM)
        dma = pltpu.SemaphoreType.DMA
        return pl.pallas_call(
            functools.partial(kernel, n_scan),
            out_shape=(
                jax.ShapeDtypeStruct(factor_w.shape, F32),
                jax.ShapeDtypeStruct(factor_h.shape, F32),
            ),
            in_specs=[pl.BlockSpec(memory_space=pl.ANY)] + [vmem] * 4,
            out_specs=(vmem, vmem),
            scratch_shapes=[
                pltpu.VMEM((groups, GROUP * FRAME, LANES), F32),
                pltpu.VMEM((3, FRAME, 8, LANES), F32),
                pltpu.VMEM((FRAME, GROUP, LANES), F32),
                pltpu.VMEM((2, FRAME + 2, GROUP, LANES), F32),
                pltpu.VMEM((EY, EX, EZ, block, frames, LANES), DATA),
                pltpu.VMEM((SLOTS, EX, block, frames, LANES), DATA),
                pltpu.VMEM((ITERS + 1, SLOTS, frames, rank), BF16),
                pltpu.VMEM((frames, rank), F32),
                pltpu.VMEM((SLOTS, frames, rank), F32),
                pltpu.VMEM((ITERS, SLOTS, frames, rank), F32),
                pltpu.VMEM((ITERS, rank, EX * pixels), BF16),
                pltpu.VMEM((comps, pixels), F32),
                pltpu.VMEM((ITERS, SLOTS, 1, rank), F32),
                pltpu.VMEM((SLOTS * frames, EX * pixels), BF16),
                pltpu.VMEM((mates, comps, pixels), F32),
                pltpu.VMEM((ITERS, mates - 1, comps, pixels), F32),
                pltpu.VMEM((ITERS, mates, 1, rank), F32),
                dma((groups,)),
                dma((groups, 2)),
                dma((groups,)),
                dma((ITERS + 1, 2)),
                dma((ITERS, 2)),
                dma((ITERS, 2)),
                dma((ITERS, 2)),
                dma((ITERS, 2)),
                dma((ITERS, 2)),
            ],
            compiler_params=pltpu.CompilerParams(
                collective_id=0, has_side_effects=True, vmem_limit_bytes=58 * 1024 * 1024
            ),
        )(raw_frames.reshape(frames * FRAME, LANES), gain_map, coupling, factor_w, factor_h)

    return jax.shard_map(
        local,
        mesh=mesh,
        in_specs=(
            P(("scan", "pix"), None, None),
            P(),
            P(),
            P(("scan", "pix"), None),
            P("scan", "pix"),
        ),
        out_specs=(P(("scan", "pix"), None), P("scan", "pix")),
        check_vma=False,
    )
```

time: 172 us -> 119 us (0.69)
  Pallas kernels: 168 us -> 115 us
    pallas_call x1, Pallas kernels: 168 us -> 115 us  [local(): pl.pallas_call(functools.partial(kernel, n_scan), out_shape=(jax.ShapeDty...]
where the time goes in v2:
time: 119 us
  Pallas kernels  115 us (97%)
  local copies, waits for them, and re-layouts  2.99 us (3%)
    pallas_call x1, Pallas kernels, local(): pl.pallas_call(functools.partial(kernel, n_scan), out_shape=(jax.ShapeDty...  115 us
    unnamed x2, local copies, waits for them, and re-layouts  2.99 us

profile of v2, /device:TPU:1, one launch (start us, length us, event | category | flops | bytes accessed | tf_op | source)
XLA Modules:
  0.0 118.5 jit_solution(8352787496951006111)
XLA Ops:
  0.6 114.9 %shard_map.68 = (f32[48,256]{1,0:T(8,128)}, f32[64,512]{1,0:T(8,128)}) custom-call(f32[6144,128]{1,0:T(8,128)} %bitcast.1, f32[128,128]{1,0:T(8,128)} %gain_ref.1, f32[128,128]{1,0:T(8,128)} %couple_ref.1, f32[48,256]{1,0:T(8,128)} %w_ref.1, f32[64,512]{1,0:T(8,128)} %h_ref.1), custom_call_target="tpu_custom_call" | custom-call | tf_op jit(solution)/shard_map/pallas_call | solution.py:387
  115.5 1.4 %copy.9 = f32[48,256]{1,0:T(8,128)} copy(f32[48,256]{1,0:T(8,128)} %get-tuple-element.4) | data formatting | bytes 98304
  117.0 1.6 %copy.10 = f32[64,512]{1,0:T(8,128)} copy(f32[64,512]{1,0:T(8,128)} %get-tuple-element.5) | data formatting | bytes 262144

commit v3 on v2

--- a/solution.py
+++ b/solution.py
@@ -40,6 +40,8 @@
     tile,
     w_all,
     w_now,
+    gain_v,
+    couple_v,
     num_send,
     num_recv,
     h_all,
@@ -47,6 +49,8 @@
     hsum_all,
     ratio,
     numh_send,
+    pair_recv,
+    pair_sum,
     numh_recv,
     wsum_all,
     raw_sem,
@@ -56,8 +60,10 @@
     num_sems,
     h_sems,
     hsum_sems,
+    pair_sems,
     numh_sems,
     wsum_sems,
+    out_sems,
 ):
     rows, rank = w_ref.shape
     comps, pixels = h_ref.shape
@@ -78,19 +84,19 @@
         other = (mx * n_scan + scan + j) % mates
         return other % n_scan, other // n_scan
 
-    def remote(src, dst, sems, to_scan, y, x, z):
+    def remote(src, dst, sems, to_scan, y, x, z, part=0):
         return pltpu.make_async_remote_copy(
             src_ref=src,
             dst_ref=dst,
             send_sem=sems.at[0],
-            recv_sem=sems.at[1],
+            recv_sem=sems.at[1 + part],
             device_id=(to_scan, (y * EX + x) * EZ + z),
             device_id_type=MESH,
         )
 
-    def to_slot(src, dst, sems, where):
+    def to_slot(src, dst, sems, where, part=0):
         y, z = where
-        return remote(src, dst, sems, scan, y, mx, z)
+        return remote(src, dst, sems, scan, y, mx, z, part)
 
     def to_mate(src, dst, sems, j):
         to_scan, x = mate(j)
@@ -104,6 +110,14 @@
             raw_ref.at[pl.ds(g * GROUP * FRAME, GROUP * FRAME)], raw_v.at[g], raw_sem.at[g]
         )
 
+    small = [
+        pltpu.make_async_copy(src, dst, raw_sem.at[groups + i])
+        for i, (src, dst) in enumerate(
+            ((w_ref, w_now), (h_ref, h_now), (gain_ref, gain_v), (couple_ref, couple_v))
+        )
+    ]
+    for copy in small:
+        copy.start()
     for g in range(groups):
         fetch(g).start()
 
@@ -123,25 +137,23 @@
             barrier, inc=1, device_id=(to_scan, (my * EX + x) * EZ + mz), device_id_type=MESH
         )
 
-    coupling = couple_ref[...]
-    inverse = 1.0 / (1.0 + 4.0 * coupling)
-    gain = gain_ref[...]
-    for i, value in enumerate((gain, gain * inverse, coupling * inverse)):
-        maps[i] = jnp.broadcast_to(value[:, None, :], (FRAME, 8, LANES))
-
-    w_now[...] = w_ref[...]
-    h_now[...] = h_ref[...]
-    w_all[0, 0] = w_ref[...].astype(BF16)
     my_comps = pl.ds(pl.multiple_of(scan * comps, comps), comps)
     my_pixels = pl.ds(pl.multiple_of(mx * pixels, pixels), pixels)
-    h_all[0, my_comps, my_pixels] = h_ref[...].astype(BF16)
+    for copy in small:
+        copy.wait()
+    w_all[0, 0] = w_now[...].astype(BF16)
+    h_all[0, my_comps, my_pixels] = h_now[...].astype(BF16)
 
     pl.semaphore_wait(barrier, SLOTS - 1 + mates - 1)
 
     def send_w(step):
         def go(slot, carry):
             to_slot(
-                w_all.at[step, 0], w_all.at[step, slot], w_sems.at[step], ahead(slot)
+                w_all.at[step, 0],
+                w_all.at[step, slot],
+                w_sems.at[step],
+                ahead(slot),
+                slot // CHUNK,
             ).start()
             return carry
 
@@ -152,8 +164,11 @@
         for j in range(1, mates):
             to_mate(own, own, h_sems.at[step], j).start()
 
-    def wait_w(step, which):
-        drain(w_all.at[step, pl.ds(1, SLOTS - 1)], w_sems.at[step, which])
+    def part_of(c, skip):
+        return pl.ds(c * CHUNK + skip, CHUNK - skip)
+
+    def wait_w(step, c, skip):
+        drain(w_all.at[step, part_of(c, skip)], w_sems.at[step, 1 + c])
 
     def wait_h(step, which):
         drain(
@@ -162,6 +177,12 @@
 
     send_h(0)
     send_w(0)
+
+    coupling = couple_v[...]
+    inverse = 1.0 / (1.0 + 4.0 * coupling)
+    gain = gain_v[...]
+    for i, value in enumerate((gain, gain * inverse, coupling * inverse)):
+        maps[i] = jnp.broadcast_to(value[:, None, :], (FRAME, 8, LANES))
 
     lane = lax.broadcasted_iota(jnp.int32, (ROWS, GROUP, LANES), 2)
     first, last = lane == 0, lane == LANES - 1
@@ -230,6 +251,7 @@
                 tile.at[slot, :, :, frames],
                 data_sems.at[g],
                 (y, z),
+                slot // CHUNK,
             ).start()
             return carry
 
@@ -237,6 +259,35 @@
 
     steps = SLOTS // CHUNK
     size = CHUNK * rows
+    cores = n_scan // 2
+    low, core = scan // cores, scan % cores
+    n_chips = EX * 2
+
+    def pair_copy(it, far, side):
+        k = far * 2 + side
+        other = (core + 1) % cores
+        there = (low + side) % 2 * cores + other
+        return remote(
+            numh_send.at[far, there],
+            pair_recv.at[it, k],
+            pair_sems.at[it, k],
+            low * cores + other,
+            my,
+            mx,
+            mz,
+        )
+
+    def chip_copy(it, far, side):
+        k = far * 2 + side
+        return remote(
+            pair_sum.at[k],
+            numh_recv.at[it, k - 1],
+            numh_sems.at[it, k],
+            (low + side) % 2 * cores + core,
+            my,
+            (mx + far) % EX,
+            mz,
+        )
     wide = EX * pixels
 
     def ratios(step_w, step_h, c):
@@ -267,15 +318,17 @@
 
         lax.fori_loop(1, SLOTS, share, 0)
         if it == 0:
-            wait_w(0, 1)
             for g in range(groups):
-                frames = pl.ds(g * GROUP, GROUP)
                 own_copy(g).wait()
-                drain(tile.at[pl.ds(1, SLOTS - 1), :, :, frames], data_sems.at[g, 1])
         else:
             drain(num_send.at[pl.ds(1, SLOTS - 1)], num_sems.at[it - 1, 0])
 
         def numerators(c, carry, skip=0):
+            if it == 0:
+                wait_w(0, c, skip)
+                for g in range(groups):
+                    frames = pl.ds(g * GROUP, GROUP)
+                    drain(tile.at[part_of(c, skip), :, :, frames], data_sems.at[g, 1 + c])
             part = lax.dot_general(
                 ratios(it, it, c),
                 h_all[it],
@@ -286,7 +339,7 @@
 
             def go(slot, carry):
                 to_slot(
-                    num_send.at[slot], num_recv.at[it, slot], num_sems.at[it], behind(slot)
+                    num_send.at[slot], num_recv.at[it, slot], num_sems.at[it], behind(slot), c
                 ).start()
                 return carry
 
@@ -298,44 +351,58 @@
         h_sum = hsum_all[it, 0]
         for slot in range(1, SLOTS):
             h_sum = h_sum + hsum_all[it, slot]
-        drain(num_recv.at[it, pl.ds(1, SLOTS - 1)], num_sems.at[it, 1])
 
         def add(slot, total):
             return total + num_recv[it, slot]
 
-        total = lax.fori_loop(1, SLOTS, add, num_send[0])
+        total = num_send[0]
+        for c in range(steps):
+            skip = int(c == 0)
+            drain(num_recv.at[it, part_of(c, skip)], num_sems.at[it, 1 + c])
+            total = lax.fori_loop(c * CHUNK + skip, (c + 1) * CHUNK, add, total)
         w_new = w_now[...] * total / h_sum
-        if it == ITERS - 1:
-            w_out[...] = w_new
         w_now[...] = w_new
         w_all[it + 1, 0] = w_new.astype(BF16)
         send_w(it + 1)
-        wait_w(it + 1, 1)
-        wsum_all[it, 0] = column_sums(
-            SLOTS * rows, w_all[it + 1].reshape(SLOTS * rows, rank), ((1,), (0,))
-        )
+        if it == ITERS - 1:
+            pltpu.make_async_copy(w_now, w_out, out_sems.at[0]).start()
+
+        def second(c, sums, skip=0):
+            wait_w(it + 1, c, skip)
+            slots = pl.ds(c * CHUNK, CHUNK)
+            w = w_all[it + 1, slots].reshape(size, rank)
+            ratio[pl.ds(c * size, size), :] = ratios(it + 1, it, c)
+            return sums + column_sums(size, w, ((1,), (0,)))
+
+        sums = second(0, jnp.zeros((1, rank), F32), skip=1)
+        wsum_all[it, 0] = lax.fori_loop(1, steps, second, sums)
         for j in range(1, mates):
             to_mate(wsum_all.at[it, 0], wsum_all.at[it, j], wsum_sems.at[it], j).start()
-
-        def second(c, carry):
-            ratio[pl.ds(c * size, size), :] = ratios(it + 1, it, c)
-            return carry
-
-        lax.fori_loop(0, steps, second, 0)
         if it > 0:
-            drain(numh_send.at[pl.ds(1, mates - 1)], numh_sems.at[it - 1, 0])
-        for x in range(EX):
-            numh_send[pl.ds(x * n_scan, n_scan)] = lax.dot_general(
+            for far in range(2):
+                for side in range(2):
+                    pair_copy(it - 1, far, side).wait_send()
+                    if far * 2 + side > 0:
+                        chip_copy(it - 1, far, side).wait_send()
+        for far in (1, 0):
+            x = (mx + far) % EX
+            part = lax.dot_general(
                 w_all[it + 1].reshape(SLOTS * rows, rank),
-                ratio[:, x * pixels : (x + 1) * pixels],
+                ratio[:, pl.ds(pl.multiple_of(x * pixels, pixels), pixels)],
                 (((0,), (0,)), ((), ())),
                 preferred_element_type=F32,
-            ).reshape(n_scan, comps, pixels)
-        for j in range(1, mates):
-            to_scan, x = mate(j)
-            to_mate(
-                numh_send.at[x * n_scan + to_scan], numh_recv.at[it, j - 1], numh_sems.at[it], j
-            ).start()
+            )
+            numh_send[far] = part.reshape(n_scan, comps, pixels)
+            for side in (1, 0):
+                pair_copy(it, far, side).start()
+        for far in (1, 0):
+            for side in (1, 0):
+                k = far * 2 + side
+                pair_copy(it, far, side).wait_recv()
+                here = (low + side) % 2 * cores + core
+                pair_sum[k] = numh_send[far, here] + pair_recv[it, k]
+                if k > 0:
+                    chip_copy(it, far, side).start()
         drain(wsum_all.at[it, pl.ds(1, mates - 1)], wsum_sems.at[it, 1])
         w_sum = wsum_all[it, 0]
         for j in range(1, mates):
@@ -347,15 +414,15 @@
             axis=1,
             keepdims=True,
         )
-        drain(numh_recv.at[it], numh_sems.at[it, 1])
-        total_h = numh_send[mx * n_scan + scan]
-        for j in range(mates - 1):
-            total_h = total_h + numh_recv[it, j]
+        total_h = pair_sum[0]
+        for far, side in ((0, 1), (1, 0), (1, 1)):
+            chip_copy(it, far, side).wait_recv()
+            total_h = total_h + numh_recv[it, far * 2 + side - 1]
         h_new = h_now[...] * total_h / w_sum
+        h_now[...] = h_new
         if it == ITERS - 1:
-            h_out[...] = h_new
+            pltpu.make_async_copy(h_now, h_out, out_sems.at[1]).start()
         else:
-            h_now[...] = h_new
             h_all[it + 1, my_comps, my_pixels] = h_new.astype(BF16)
             send_h(it + 1)
 
@@ -363,13 +430,19 @@
         frames = pl.ds(g * GROUP, GROUP)
         drain(tile.at[pl.ds(1, SLOTS - 1), :, :, frames], data_sems.at[g, 0])
     for step in range(ITERS + 1):
-        wait_w(step, 0)
+        drain(w_all.at[step, pl.ds(1, SLOTS - 1)], w_sems.at[step, 0])
     for step in range(ITERS):
         wait_h(step, 0)
         drain(hsum_all.at[step, pl.ds(1, SLOTS - 1)], hsum_sems.at[step, 0])
         drain(wsum_all.at[step, pl.ds(1, mates - 1)], wsum_sems.at[step, 0])
     drain(num_send.at[pl.ds(1, SLOTS - 1)], num_sems.at[ITERS - 1, 0])
-    drain(numh_send.at[pl.ds(1, mates - 1)], numh_sems.at[ITERS - 1, 0])
+    for far in range(2):
+        for side in range(2):
+            pair_copy(ITERS - 1, far, side).wait_send()
+            if far * 2 + side > 0:
+                chip_copy(ITERS - 1, far, side).wait_send()
+    pltpu.make_async_copy(w_now, w_out, out_sems.at[0]).wait()
+    pltpu.make_async_copy(h_now, h_out, out_sems.at[1]).wait()
 
 
 def solution(mesh):
@@ -382,7 +455,8 @@
         comps, pixels = factor_h.shape
         groups = frames // GROUP
         block = pixels // FRAME
-        vmem = pl.BlockSpec(memory_space=pltpu.VMEM)
+        steps = SLOTS // CHUNK
+        hbm = pl.BlockSpec(memory_space=pl.ANY)
         dma = pltpu.SemaphoreType.DMA
         return pl.pallas_call(
             functools.partial(kernel, n_scan),
@@ -390,8 +464,8 @@
                 jax.ShapeDtypeStruct(factor_w.shape, F32),
                 jax.ShapeDtypeStruct(factor_h.shape, F32),
             ),
-            in_specs=[pl.BlockSpec(memory_space=pl.ANY)] + [vmem] * 4,
-            out_specs=(vmem, vmem),
+            in_specs=[hbm] * 5,
+            out_specs=(hbm, hbm),
             scratch_shapes=[
                 pltpu.VMEM((groups, GROUP * FRAME, LANES), F32),
                 pltpu.VMEM((3, FRAME, 8, LANES), F32),
@@ -401,24 +475,30 @@
                 pltpu.VMEM((SLOTS, EX, block, frames, LANES), DATA),
                 pltpu.VMEM((ITERS + 1, SLOTS, frames, rank), BF16),
                 pltpu.VMEM((frames, rank), F32),
+                pltpu.VMEM((FRAME, LANES), F32),
+                pltpu.VMEM((FRAME, LANES), F32),
                 pltpu.VMEM((SLOTS, frames, rank), F32),
                 pltpu.VMEM((ITERS, SLOTS, frames, rank), F32),
                 pltpu.VMEM((ITERS, rank, EX * pixels), BF16),
                 pltpu.VMEM((comps, pixels), F32),
                 pltpu.VMEM((ITERS, SLOTS, 1, rank), F32),
                 pltpu.VMEM((SLOTS * frames, EX * pixels), BF16),
-                pltpu.VMEM((mates, comps, pixels), F32),
-                pltpu.VMEM((ITERS, mates - 1, comps, pixels), F32),
+                pltpu.VMEM((EX, n_scan, comps, pixels), F32),
+                pltpu.VMEM((ITERS, mates // 2, comps, pixels), F32),
+                pltpu.VMEM((mates // 2, comps, pixels), F32),
+                pltpu.VMEM((ITERS, mates // 2 - 1, comps, pixels), F32),
                 pltpu.VMEM((ITERS, mates, 1, rank), F32),
+                dma((groups + 4,)),
+                dma((groups, 1 + steps)),
                 dma((groups,)),
-                dma((groups, 2)),
-                dma((groups,)),
-                dma((ITERS + 1, 2)),
+                dma((ITERS + 1, 1 + steps)),
+                dma((ITERS, 1 + steps)),
                 dma((ITERS, 2)),
                 dma((ITERS, 2)),
+                dma((ITERS, mates // 2, 2)),
+                dma((ITERS, mates // 2, 2)),
                 dma((ITERS, 2)),
-                dma((ITERS, 2)),
-                dma((ITERS, 2)),
+                dma((2,)),
             ],
             compiler_params=pltpu.CompilerParams(
                 collective_id=0, has_side_effects=True, vmem_limit_bytes=58 * 1024 * 1024

time: 119 us -> 109 us (0.916)
  Pallas kernels: 115 us -> 105 us
    pallas_call x1, Pallas kernels: 115 us -> 105 us  [local(): pl.pallas_call(functools.partial(kernel, n_scan), out_shape=(jax.ShapeDty...]
where the time goes in v3:
time: 109 us
  Pallas kernels  105 us (96%)
  local copies, waits for them, and re-layouts  2.99 us (3%)
    pallas_call x1, Pallas kernels, local(): pl.pallas_call(functools.partial(kernel, n_scan), out_shape=(jax.ShapeDty...  105 us
    unnamed x2, local copies, waits for them, and re-layouts  2.99 us

profile of v3, /device:TPU:1, one launch (start us, length us, event | category | flops | bytes accessed | tf_op | source)
XLA Modules:
  0.0 108.7 jit_solution(7311431568637095014)
XLA Ops:
  0.6 105.1 %shard_map.68 = (f32[48,256]{1,0:T(8,128)}, f32[64,512]{1,0:T(8,128)}) custom-call(f32[6144,128]{1,0:T(8,128)} %bitcast.1, f32[128,128]{1,0:T(8,128)} %gain_ref.1, f32[128,128]{1,0:T(8,128)} %couple_ref.1, f32[48,256]{1,0:T(8,128)} %w_ref.1, f32[64,512]{1,0:T(8,128)} %h_ref.1), custom_call_target="tpu_custom_call" | custom-call | tf_op jit(solution)/shard_map/pallas_call | solution.py:461
  105.7 1.4 %copy.9 = f32[48,256]{1,0:T(8,128)} copy(f32[48,256]{1,0:T(8,128)} %get-tuple-element.4) | data formatting | bytes 98304
  107.1 1.6 %copy.10 = f32[64,512]{1,0:T(8,128)} copy(f32[64,512]{1,0:T(8,128)} %get-tuple-element.5) | data formatting | bytes 262144

commit v4 on v3

--- a/solution.py
+++ b/solution.py
@@ -16,7 +16,9 @@
 GROUP = 16
 ROWS = 64
 DATA = jnp.bfloat16
-CHUNK = 4
+PARTS = ((0, 2 * GROUP), (2 * GROUP, GROUP))
+UNITS = ((0, 0, SLOTS // 2), (0, SLOTS // 2, SLOTS // 2), (1, 0, SLOTS))
+HALF = SLOTS // 2
 
 MESH = pl.DeviceIdType.MESH
 F32 = jnp.float32
@@ -38,12 +40,15 @@
     field,
     charge,
     tile,
-    w_all,
+    w_first,
+    w_second,
     w_now,
     gain_v,
     couple_v,
-    num_send,
-    num_recv,
+    num_send_first,
+    num_send_second,
+    num_recv_first,
+    num_recv_second,
     h_all,
     h_now,
     hsum_all,
@@ -59,6 +64,7 @@
     w_sems,
     num_sems,
     h_sems,
+    h_pair_sems,
     hsum_sems,
     pair_sems,
     numh_sems,
@@ -70,9 +76,15 @@
     block = pixels // FRAME
     groups = rows // GROUP
     mates = EX * n_scan
+    w_all = (w_first, w_second)
+    num_send = (num_send_first, num_send_second)
+    num_recv = (num_recv_first, num_recv_second)
     scan = lax.axis_index("scan")
     pix = lax.axis_index("pix")
     my, mx, mz = pix // (EX * EZ), (pix // EZ) % EX, pix % EZ
+    cores = n_scan // 2
+    low, core = scan // cores, scan % cores
+    twin = (core + 1) % cores
 
     def ahead(slot):
         return (my + slot // EZ) % EY, (mz + slot % EZ) % EZ
@@ -137,46 +149,89 @@
             barrier, inc=1, device_id=(to_scan, (my * EX + x) * EZ + mz), device_id_type=MESH
         )
 
-    my_comps = pl.ds(pl.multiple_of(scan * comps, comps), comps)
-    my_pixels = pl.ds(pl.multiple_of(mx * pixels, pixels), pixels)
     for copy in small:
         copy.wait()
-    w_all[0, 0] = w_now[...].astype(BF16)
-    h_all[0, my_comps, my_pixels] = h_now[...].astype(BF16)
-
-    pl.semaphore_wait(barrier, SLOTS - 1 + mates - 1)
-
-    def send_w(step):
-        def go(slot, carry):
-            to_slot(
-                w_all.at[step, 0],
-                w_all.at[step, slot],
-                w_sems.at[step],
-                ahead(slot),
-                slot // CHUNK,
-            ).start()
-            return carry
-
-        lax.fori_loop(1, SLOTS, go, 0)
+
+    def part_rows(p):
+        return pl.ds(*PARTS[p])
+
+    def send_w(step, p):
+        for copy_slots in ((1, HALF), (HALF, SLOTS)):
+
+            def go(slot, carry):
+                to_slot(
+                    w_all[p].at[step, 0],
+                    w_all[p].at[step, slot],
+                    w_sems.at[step, p],
+                    ahead(slot),
+                    copy_slots[0] // HALF,
+                ).start()
+                return carry
+
+            lax.fori_loop(*copy_slots, go, 0)
+
+    def halves(u):
+        _, start, count = UNITS[u]
+        both = ((1, HALF - 1, 0), (HALF, HALF, 1))
+        return [h for h in both if start <= h[0] < start + count]
+
+    def wait_w(step, u):
+        p = UNITS[u][0]
+        for start, count, half in halves(u):
+            drain(w_all[p].at[step, pl.ds(start, count)], w_sems.at[step, p, 1 + half])
+
+    def place(far, side, of_core):
+        at = (low + side) % 2 * cores + of_core
+        return (
+            pl.ds(pl.multiple_of(at * comps, comps), comps),
+            pl.ds(pl.multiple_of((mx + far) % EX * pixels, pixels), pixels),
+        )
+
+    mine = place(0, 0, core)
+
+    def h_chip(step, far, side):
+        own = h_all.at[step, mine[0], mine[1]]
+        return remote(
+            own,
+            own,
+            h_sems.at[step, far * 2 + side],
+            (low + side) % 2 * cores + core,
+            my,
+            (mx + far) % EX,
+            mz,
+        )
+
+    def h_pair(step, far, side):
+        at = place(far, side, core)
+        part = h_all.at[step, at[0], at[1]]
+        return remote(
+            part, part, h_pair_sems.at[step, far * 2 + side], low * cores + twin, my, mx, mz
+        )
+
+    others = ((1, 0), (1, 1), (0, 1))
+    every = ((0, 0),) + others
 
     def send_h(step):
-        own = h_all.at[step, my_comps, my_pixels]
-        for j in range(1, mates):
-            to_mate(own, own, h_sems.at[step], j).start()
-
-    def part_of(c, skip):
-        return pl.ds(c * CHUNK + skip, CHUNK - skip)
-
-    def wait_w(step, c, skip):
-        drain(w_all.at[step, part_of(c, skip)], w_sems.at[step, 1 + c])
-
-    def wait_h(step, which):
-        drain(
-            h_all.at[step, pl.ds(0, rank * (mates - 1) // mates)], h_sems.at[step, which]
-        )
-
-    send_h(0)
-    send_w(0)
+        for far, side in others:
+            h_chip(step, far, side).start()
+        h_pair(step, 0, 0).start()
+
+    def finish_h(step):
+        for far, side in others[::-1]:
+            h_chip(step, far, side).wait_recv()
+            h_pair(step, far, side).start()
+        for far, side in every:
+            h_pair(step, far, side).wait_recv()
+
+    for p in range(2):
+        w_all[p][0, 0] = w_now[part_rows(p), :].astype(BF16)
+    h_all[0, mine[0], mine[1]] = h_now[...].astype(BF16)
+
+    def meet():
+        pl.semaphore_wait(barrier, SLOTS - 1 + mates - 1)
+        send_h(0)
+        for p in range(2):
+            send_w(0, p)
 
     coupling = couple_v[...]
     inverse = 1.0 / (1.0 + 4.0 * coupling)
@@ -192,7 +247,7 @@
         field[i, 0] = edge
         field[i, FRAME + 1] = edge
 
-    def correct(g):
+    def correct(g, between=None):
         def map_rows(i, at):
             value = maps[i, pl.ds(at, ROWS)]
             return jnp.concatenate([value] * (GROUP // 8), axis=1)
@@ -231,6 +286,8 @@
                 return carry
 
             lax.fori_loop(0, FRAME // ROWS, sweep, 0)
+            if s == 1 and between is not None:
+                between()
 
     def own_copy(g):
         frames = pl.ds(g * GROUP, GROUP)
@@ -240,38 +297,37 @@
 
     for g in range(groups):
         fetch(g).wait()
-        correct(g)
+        correct(g, meet if g == 0 else None)
         own_copy(g).start()
         frames = pl.ds(g * GROUP, GROUP)
 
-        def go(slot, carry):
-            y, z = ahead(slot)
-            to_slot(
-                charge.at[y, :, z, :, frames],
-                tile.at[slot, :, :, frames],
-                data_sems.at[g],
-                (y, z),
-                slot // CHUNK,
-            ).start()
-            return carry
-
-        lax.fori_loop(1, SLOTS, go, 0)
-
-    steps = SLOTS // CHUNK
-    size = CHUNK * rows
-    cores = n_scan // 2
-    low, core = scan // cores, scan % cores
-    n_chips = EX * 2
+        for half, (start, stop) in enumerate(((1, HALF), (HALF, SLOTS))):
+
+            def go(slot, carry):
+                y, z = ahead(slot)
+                to_slot(
+                    charge.at[y, :, z, :, frames],
+                    tile.at[slot, :, :, frames],
+                    data_sems.at[g],
+                    (y, z),
+                    half,
+                ).start()
+                return carry
+
+            lax.fori_loop(start, stop, go, 0)
+
+    wide = EX * pixels
+    unit_rows = [count * PARTS[p][1] for p, _, count in UNITS]
+    unit_start = [sum(unit_rows[:u]) for u in range(len(UNITS))]
 
     def pair_copy(it, far, side):
         k = far * 2 + side
-        other = (core + 1) % cores
-        there = (low + side) % 2 * cores + other
+        there = (low + side) % 2 * cores + twin
         return remote(
             numh_send.at[far, there],
             pair_recv.at[it, k],
             pair_sems.at[it, k],
-            low * cores + other,
+            low * cores + twin,
             my,
             mx,
             mz,
@@ -290,111 +346,124 @@
         )
     wide = EX * pixels
 
-    def ratios(step_w, step_h, c):
-        slots = pl.ds(c * CHUNK, CHUNK)
-        w = w_all[step_w, slots].reshape(size, rank)
-        product = jnp.dot(w, h_all[step_h], preferred_element_type=F32)
+    def wait_data(u):
+        p, start, _ = UNITS[u]
+        first_frame, count = PARTS[p]
+        for g in range(first_frame // GROUP, (first_frame + count) // GROUP):
+            frames = pl.ds(g * GROUP, GROUP)
+            if start == 0:
+                own_copy(g).wait()
+            for at, n, half in halves(u):
+                drain(tile.at[pl.ds(at, n), :, :, frames], data_sems.at[g, 1 + half])
+
+    def unit_w(step, u):
+        p, start, count = UNITS[u]
+        return w_all[p][step, pl.ds(start, count)].reshape(unit_rows[u], rank)
+
+    def ratios(step_w, step_h, u):
+        p, start, count = UNITS[u]
+        slots = pl.ds(start, count)
+        product = jnp.dot(unit_w(step_w, u), h_all[step_h], preferred_element_type=F32)
         parts = []
         for x in range(EX):
             for k in range(block):
                 at = (x * block + k) * LANES
-                data = tile[slots, x, k].reshape(size, LANES).astype(F32)
+                data = tile[slots, x, k, part_rows(p)].reshape(unit_rows[u], LANES).astype(F32)
                 parts.append((data / product[:, at : at + LANES]).astype(BF16))
         return jnp.concatenate(parts, axis=1)
 
-    def column_sums(lhs_rows, operand, dims):
-        ones = jnp.ones((8, lhs_rows), BF16)
-        return lax.dot_general(ones, operand, (dims, ((), ())), preferred_element_type=F32)[:1]
-
     for it in range(ITERS):
-        wait_h(it, 1)
-        hsum_all[it, 0] = column_sums(wide, h_all[it], ((1,), (1,)))
-
-        def share(slot, carry):
-            to_slot(
-                hsum_all.at[it, 0], hsum_all.at[it, slot], hsum_sems.at[it], ahead(slot)
-            ).start()
-            return carry
-
-        lax.fori_loop(1, SLOTS, share, 0)
-        if it == 0:
-            for g in range(groups):
-                own_copy(g).wait()
-        else:
-            drain(num_send.at[pl.ds(1, SLOTS - 1)], num_sems.at[it - 1, 0])
-
-        def numerators(c, carry, skip=0):
+        finish_h(it)
+        for u, (p, start, count) in enumerate(UNITS):
             if it == 0:
-                wait_w(0, c, skip)
-                for g in range(groups):
-                    frames = pl.ds(g * GROUP, GROUP)
-                    drain(tile.at[part_of(c, skip), :, :, frames], data_sems.at[g, 1 + c])
-            part = lax.dot_general(
-                ratios(it, it, c),
-                h_all[it],
-                (((1,), (1,)), ((), ())),
-                preferred_element_type=F32,
+                wait_w(0, u)
+                wait_data(u)
+            elif start == 0:
+                drain(num_send[p].at[pl.ds(1, SLOTS - 1)], num_sems.at[it - 1, p, 0])
+            terms = ratios(it, it, u)
+            if u == 0:
+                terms = jnp.concatenate([terms, jnp.ones((16, wide), BF16)], axis=0)
+            terms = lax.dot_general(
+                terms, h_all[it], (((1,), (1,)), ((), ())), preferred_element_type=F32
             )
-            num_send[pl.ds(c * CHUNK, CHUNK)] = part.reshape(CHUNK, rows, rank)
+            num_send[p][pl.ds(start, count)] = terms[: unit_rows[u]].reshape(
+                count, PARTS[p][1], rank
+            )
 
             def go(slot, carry):
                 to_slot(
-                    num_send.at[slot], num_recv.at[it, slot], num_sems.at[it], behind(slot), c
+                    num_send[p].at[slot],
+                    num_recv[p].at[it, slot],
+                    num_sems.at[it, p],
+                    behind(slot),
                 ).start()
                 return carry
 
-            return lax.fori_loop(c * CHUNK + skip, (c + 1) * CHUNK, go, carry)
-
-        numerators(0, 0, skip=1)
-        lax.fori_loop(1, steps, numerators, 0)
+            lax.fori_loop(max(start, 1), start + count, go, 0)
+            if u == 0:
+                hsum_all[it, 0] = terms[unit_rows[u] : unit_rows[u] + 1]
+
+                def share(slot, carry):
+                    to_slot(
+                        hsum_all.at[it, 0], hsum_all.at[it, slot], hsum_sems.at[it], ahead(slot)
+                    ).start()
+                    return carry
+
+                lax.fori_loop(1, SLOTS, share, 0)
+
         drain(hsum_all.at[it, pl.ds(1, SLOTS - 1)], hsum_sems.at[it, 1])
         h_sum = hsum_all[it, 0]
         for slot in range(1, SLOTS):
             h_sum = h_sum + hsum_all[it, slot]
-
-        def add(slot, total):
-            return total + num_recv[it, slot]
-
-        total = num_send[0]
-        for c in range(steps):
-            skip = int(c == 0)
-            drain(num_recv.at[it, part_of(c, skip)], num_sems.at[it, 1 + c])
-            total = lax.fori_loop(c * CHUNK + skip, (c + 1) * CHUNK, add, total)
-        w_new = w_now[...] * total / h_sum
-        w_now[...] = w_new
-        w_all[it + 1, 0] = w_new.astype(BF16)
-        send_w(it + 1)
+        for p in range(2):
+            drain(num_recv[p].at[it, pl.ds(1, SLOTS - 1)], num_sems.at[it, p, 1])
+
+            def add(slot, total):
+                return total + num_recv[p][it, slot]
+
+            total = lax.fori_loop(1, SLOTS, add, num_send[p][0])
+            w_new = w_now[part_rows(p), :] * total / h_sum
+            w_now[part_rows(p), :] = w_new
+            w_all[p][it + 1, 0] = w_new.astype(BF16)
+            send_w(it + 1, p)
         if it == ITERS - 1:
             pltpu.make_async_copy(w_now, w_out, out_sems.at[0]).start()
 
-        def second(c, sums, skip=0):
-            wait_w(it + 1, c, skip)
-            slots = pl.ds(c * CHUNK, CHUNK)
-            w = w_all[it + 1, slots].reshape(size, rank)
-            ratio[pl.ds(c * size, size), :] = ratios(it + 1, it, c)
-            return sums + column_sums(size, w, ((1,), (0,)))
-
-        sums = second(0, jnp.zeros((1, rank), F32), skip=1)
-        wsum_all[it, 0] = lax.fori_loop(1, steps, second, sums)
+        if it > 0:
+            for far, side in every:
+                pair_copy(it - 1, far, side).wait_send()
+            for far, side in others:
+                chip_copy(it - 1, far, side).wait_send()
+
+        def component_terms(p, far):
+            units = [u for u in range(len(UNITS)) if UNITS[u][0] == p]
+            count = SLOTS * PARTS[p][1]
+            x = (mx + far) % EX
+            return lax.dot_general(
+                w_all[p][it + 1].reshape(count, rank),
+                ratio[
+                    pl.ds(unit_start[units[0]], count),
+                    pl.ds(pl.multiple_of(x * pixels, pixels), pixels),
+                ],
+                (((0,), (0,)), ((), ())),
+                preferred_element_type=F32,
+            ).reshape(n_scan, comps, pixels)
+
+        w_sum = jnp.zeros((1, rank), F32)
+        for u in range(len(UNITS)):
+            wait_w(it + 1, u)
+            ratio[pl.ds(unit_start[u], unit_rows[u]), :] = ratios(it + 1, it, u)
+            w_sum = w_sum + jnp.sum(unit_w(it + 1, u).astype(F32), axis=0, keepdims=True)
+            if u == 1:
+                for far in (1, 0):
+                    numh_send[far] = component_terms(0, far)
+        wsum_all[it, 0] = w_sum
+        for far in (1, 0):
+            numh_send[far] = numh_send[far] + component_terms(1, far)
+            for side in (1, 0):
+                pair_copy(it, far, side).start()
         for j in range(1, mates):
             to_mate(wsum_all.at[it, 0], wsum_all.at[it, j], wsum_sems.at[it], j).start()
-        if it > 0:
-            for far in range(2):
-                for side in range(2):
-                    pair_copy(it - 1, far, side).wait_send()
-                    if far * 2 + side > 0:
-                        chip_copy(it - 1, far, side).wait_send()
-        for far in (1, 0):
-            x = (mx + far) % EX
-            part = lax.dot_general(
-                w_all[it + 1].reshape(SLOTS * rows, rank),
-                ratio[:, pl.ds(pl.multiple_of(x * pixels, pixels), pixels)],
-                (((0,), (0,)), ((), ())),
-                preferred_element_type=F32,
-            )
-            numh_send[far] = part.reshape(n_scan, comps, pixels)
-            for side in (1, 0):
-                pair_copy(it, far, side).start()
         for far in (1, 0):
             for side in (1, 0):
                 k = far * 2 + side
@@ -423,24 +492,28 @@
         if it == ITERS - 1:
             pltpu.make_async_copy(h_now, h_out, out_sems.at[1]).start()
         else:
-            h_all[it + 1, my_comps, my_pixels] = h_new.astype(BF16)
+            h_all[it + 1, mine[0], mine[1]] = h_new.astype(BF16)
             send_h(it + 1)
 
     for g in range(groups):
         frames = pl.ds(g * GROUP, GROUP)
         drain(tile.at[pl.ds(1, SLOTS - 1), :, :, frames], data_sems.at[g, 0])
     for step in range(ITERS + 1):
-        drain(w_all.at[step, pl.ds(1, SLOTS - 1)], w_sems.at[step, 0])
+        for p in range(2):
+            drain(w_all[p].at[step, pl.ds(1, SLOTS - 1)], w_sems.at[step, p, 0])
     for step in range(ITERS):
-        wait_h(step, 0)
+        for far, side in others:
+            h_chip(step, far, side).wait_send()
+        for far, side in every:
+            h_pair(step, far, side).wait_send()
         drain(hsum_all.at[step, pl.ds(1, SLOTS - 1)], hsum_sems.at[step, 0])
         drain(wsum_all.at[step, pl.ds(1, mates - 1)], wsum_sems.at[step, 0])
-    drain(num_send.at[pl.ds(1, SLOTS - 1)], num_sems.at[ITERS - 1, 0])
-    for far in range(2):
-        for side in range(2):
-            pair_copy(ITERS - 1, far, side).wait_send()
-            if far * 2 + side > 0:
-                chip_copy(ITERS - 1, far, side).wait_send()
+    for p in range(2):
+        drain(num_send[p].at[pl.ds(1, SLOTS - 1)], num_sems.at[ITERS - 1, p, 0])
+    for far, side in every:
+        pair_copy(ITERS - 1, far, side).wait_send()
+    for far, side in others:
+        chip_copy(ITERS - 1, far, side).wait_send()
     pltpu.make_async_copy(w_now, w_out, out_sems.at[0]).wait()
     pltpu.make_async_copy(h_now, h_out, out_sems.at[1]).wait()
 
@@ -455,7 +528,6 @@
         comps, pixels = factor_h.shape
         groups = frames // GROUP
         block = pixels // FRAME
-        steps = SLOTS // CHUNK
         hbm = pl.BlockSpec(memory_space=pl.ANY)
         dma = pltpu.SemaphoreType.DMA
         return pl.pallas_call(
@@ -473,12 +545,12 @@
                 pltpu.VMEM((2, FRAME + 2, GROUP, LANES), F32),
                 pltpu.VMEM((EY, EX, EZ, block, frames, LANES), DATA),
                 pltpu.VMEM((SLOTS, EX, block, frames, LANES), DATA),
-                pltpu.VMEM((ITERS + 1, SLOTS, frames, rank), BF16),
+                *[pltpu.VMEM((ITERS + 1, SLOTS, n, rank), BF16) for _, n in PARTS],
                 pltpu.VMEM((frames, rank), F32),
                 pltpu.VMEM((FRAME, LANES), F32),
                 pltpu.VMEM((FRAME, LANES), F32),
-                pltpu.VMEM((SLOTS, frames, rank), F32),
-                pltpu.VMEM((ITERS, SLOTS, frames, rank), F32),
+                *[pltpu.VMEM((SLOTS, n, rank), F32) for _, n in PARTS],
+                *[pltpu.VMEM((ITERS, SLOTS, n, rank), F32) for _, n in PARTS],
                 pltpu.VMEM((ITERS, rank, EX * pixels), BF16),
                 pltpu.VMEM((comps, pixels), F32),
                 pltpu.VMEM((ITERS, SLOTS, 1, rank), F32),
@@ -489,11 +561,12 @@
                 pltpu.VMEM((ITERS, mates // 2 - 1, comps, pixels), F32),
                 pltpu.VMEM((ITERS, mates, 1, rank), F32),
                 dma((groups + 4,)),
-                dma((groups, 1 + steps)),
+                dma((groups, 3)),
                 dma((groups,)),
-                dma((ITERS + 1, 1 + steps)),
-                dma((ITERS, 1 + steps)),
-                dma((ITERS, 2)),
+                dma((ITERS + 1, 2, 3)),
+                dma((ITERS, 2, 2)),
+                dma((ITERS, mates // 2, 2)),
+                dma((ITERS, mates // 2, 2)),
                 dma((ITERS, 2)),
                 dma((ITERS, mates // 2, 2)),
                 dma((ITERS, mates // 2, 2)),

time: 109 us -> 98.1 us (0.90)
  Pallas kernels: 105 us -> 94.2 us
    pallas_call x1, Pallas kernels: 105 us -> 94.2 us  [local(): pl.pallas_call(functools.partial(kernel, n_scan), out_shape=(jax.ShapeDty...]
where the time goes in v4:
time: 98.1 us; the launch traced here: 97.9 us
  Pallas kernels  94.2 us (96%)
  local copies, waits for them, and re-layouts  2.99 us (3%)
    pallas_call x1, Pallas kernels, local(): pl.pallas_call(functools.partial(kernel, n_scan), out_shape=(jax.ShapeDty...  94.2 us
    unnamed x2, local copies, waits for them, and re-layouts  2.99 us

profile of v4, /device:TPU:1, one launch (start us, length us, event | category | flops | bytes accessed | tf_op | source)
XLA Modules:
  0.0 97.9 jit_solution(12889218304250063754)
XLA Ops:
  0.6 94.2 %shard_map.68 = (f32[48,256]{1,0:T(8,128)}, f32[64,512]{1,0:T(8,128)}) custom-call(f32[6144,128]{1,0:T(8,128)} %bitcast.1, f32[128,128]{1,0:T(8,128)} %gain_ref.1, f32[128,128]{1,0:T(8,128)} %couple_ref.1, f32[48,256]{1,0:T(8,128)} %w_ref.1, f32[64,512]{1,0:T(8,128)} %h_ref.1), custom_call_target="tpu_custom_call" | custom-call | tf_op jit(solution)/shard_map/pallas_call | solution.py:533
  94.9 1.4 %copy.9 = f32[48,256]{1,0:T(8,128)} copy(f32[48,256]{1,0:T(8,128)} %get-tuple-element.4) | data formatting | bytes 98304
  96.3 1.6 %copy.10 = f32[64,512]{1,0:T(8,128)} copy(f32[64,512]{1,0:T(8,128)} %get-tuple-element.5) | data formatting | bytes 262144

commit v5 on v4

--- a/solution.py
+++ b/solution.py
@@ -16,8 +16,8 @@
 GROUP = 16
 ROWS = 64
 DATA = jnp.bfloat16
-PARTS = ((0, 2 * GROUP), (2 * GROUP, GROUP))
-UNITS = ((0, 0, SLOTS // 2), (0, SLOTS // 2, SLOTS // 2), (1, 0, SLOTS))
+PARTS = tuple((g * GROUP, GROUP) for g in range(3))
+UNITS = tuple((g, 0, SLOTS) for g in range(3))
 HALF = SLOTS // 2
 
 MESH = pl.DeviceIdType.MESH
@@ -38,17 +38,15 @@
     maps,
     scaled,
     field,
+    stretch,
     charge,
     tile,
-    w_first,
-    w_second,
+    w_all,
     w_now,
     gain_v,
     couple_v,
-    num_send_first,
-    num_send_second,
-    num_recv_first,
-    num_recv_second,
+    num_send,
+    num_recv,
     h_all,
     h_now,
     hsum_all,
@@ -69,16 +67,12 @@
     pair_sems,
     numh_sems,
     wsum_sems,
-    out_sems,
 ):
     rows, rank = w_ref.shape
     comps, pixels = h_ref.shape
     block = pixels // FRAME
     groups = rows // GROUP
     mates = EX * n_scan
-    w_all = (w_first, w_second)
-    num_send = (num_send_first, num_send_second)
-    num_recv = (num_recv_first, num_recv_second)
     scan = lax.axis_index("scan")
     pix = lax.axis_index("pix")
     my, mx, mz = pix // (EX * EZ), (pix // EZ) % EX, pix % EZ
@@ -223,14 +217,14 @@
         for far, side in every:
             h_pair(step, far, side).wait_recv()
 
-    for p in range(2):
+    for p in range(len(PARTS)):
         w_all[p][0, 0] = w_now[part_rows(p), :].astype(BF16)
     h_all[0, mine[0], mine[1]] = h_now[...].astype(BF16)
 
     def meet():
         pl.semaphore_wait(barrier, SLOTS - 1 + mates - 1)
         send_h(0)
-        for p in range(2):
+        for p in range(len(PARTS)):
             send_w(0, p)
 
     coupling = couple_v[...]
@@ -238,6 +232,13 @@
     gain = gain_v[...]
     for i, value in enumerate((gain, gain * inverse, coupling * inverse)):
         maps[i] = jnp.broadcast_to(value[:, None, :], (FRAME, 8, LANES))
+
+    shape = (block, rows, LANES)
+    turn = [lax.broadcasted_iota(jnp.int32, shape, i) for i in range(3)]
+    turn = jnp.bitwise_and(107 * turn[0] + 193 * turn[1] + 145 * turn[2], 255)
+    factor = 1.0 + (turn.astype(F32) - 127.5) * (2.0**-12)
+    stretch[0] = factor
+    stretch[1] = 1.0 / factor
 
     lane = lax.broadcasted_iota(jnp.int32, (ROWS, GROUP, LANES), 2)
     first, last = lane == 0, lane == LANES - 1
@@ -278,8 +279,11 @@
                 )
                 if s == SWEEPS - 1:
                     slabs = ROWS // (EX * EZ * block)
-                    charge[pl.ds(c * slabs, slabs), :, :, :, pl.ds(g * GROUP, GROUP), :] = (
-                        value.astype(charge.dtype).reshape(slabs, EX, EZ, block, GROUP, LANES)
+                    frames = pl.ds(g * GROUP, GROUP)
+                    value = value.reshape(slabs * EX * EZ, block, GROUP, LANES)
+                    value = (value * stretch[0, :, frames][None]).astype(charge.dtype)
+                    charge[pl.ds(c * slabs, slabs), :, :, :, frames, :] = value.reshape(
+                        slabs, EX, EZ, block, GROUP, LANES
                     )
                 else:
                     field[(s + 1) % 2, pl.ds(at + 1, ROWS)] = value
@@ -368,7 +372,8 @@
         for x in range(EX):
             for k in range(block):
                 at = (x * block + k) * LANES
-                data = tile[slots, x, k, part_rows(p)].reshape(unit_rows[u], LANES).astype(F32)
+                data = tile[slots, x, k, part_rows(p)].astype(F32) * stretch[1, k, part_rows(p)][None]
+                data = data.reshape(unit_rows[u], LANES)
                 parts.append((data / product[:, at : at + LANES]).astype(BF16))
         return jnp.concatenate(parts, axis=1)
 
@@ -415,7 +420,7 @@
         h_sum = hsum_all[it, 0]
         for slot in range(1, SLOTS):
             h_sum = h_sum + hsum_all[it, slot]
-        for p in range(2):
+        for p in range(len(PARTS)):
             drain(num_recv[p].at[it, pl.ds(1, SLOTS - 1)], num_sems.at[it, p, 1])
 
             def add(slot, total):
@@ -427,7 +432,7 @@
             w_all[p][it + 1, 0] = w_new.astype(BF16)
             send_w(it + 1, p)
         if it == ITERS - 1:
-            pltpu.make_async_copy(w_now, w_out, out_sems.at[0]).start()
+            w_out[...] = w_now[...]
 
         if it > 0:
             for far, side in every:
@@ -454,12 +459,14 @@
             wait_w(it + 1, u)
             ratio[pl.ds(unit_start[u], unit_rows[u]), :] = ratios(it + 1, it, u)
             w_sum = w_sum + jnp.sum(unit_w(it + 1, u).astype(F32), axis=0, keepdims=True)
-            if u == 1:
+            p = UNITS[u][0]
+            if p < len(PARTS) - 1 and UNITS[u + 1][0] > p:
                 for far in (1, 0):
-                    numh_send[far] = component_terms(0, far)
+                    terms = component_terms(p, far)
+                    numh_send[far] = terms if p == 0 else numh_send[far] + terms
         wsum_all[it, 0] = w_sum
         for far in (1, 0):
-            numh_send[far] = numh_send[far] + component_terms(1, far)
+            numh_send[far] = numh_send[far] + component_terms(len(PARTS) - 1, far)
             for side in (1, 0):
                 pair_copy(it, far, side).start()
         for j in range(1, mates):
@@ -488,10 +495,10 @@
             chip_copy(it, far, side).wait_recv()
             total_h = total_h + numh_recv[it, far * 2 + side - 1]
         h_new = h_now[...] * total_h / w_sum
-        h_now[...] = h_new
         if it == ITERS - 1:
-            pltpu.make_async_copy(h_now, h_out, out_sems.at[1]).start()
+            h_out[...] = h_new
         else:
+            h_now[...] = h_new
             h_all[it + 1, mine[0], mine[1]] = h_new.astype(BF16)
             send_h(it + 1)
 
@@ -499,7 +506,7 @@
         frames = pl.ds(g * GROUP, GROUP)
         drain(tile.at[pl.ds(1, SLOTS - 1), :, :, frames], data_sems.at[g, 0])
     for step in range(ITERS + 1):
-        for p in range(2):
+        for p in range(len(PARTS)):
             drain(w_all[p].at[step, pl.ds(1, SLOTS - 1)], w_sems.at[step, p, 0])
     for step in range(ITERS):
         for far, side in others:
@@ -508,14 +515,12 @@
             h_pair(step, far, side).wait_send()
         drain(hsum_all.at[step, pl.ds(1, SLOTS - 1)], hsum_sems.at[step, 0])
         drain(wsum_all.at[step, pl.ds(1, mates - 1)], wsum_sems.at[step, 0])
-    for p in range(2):
+    for p in range(len(PARTS)):
         drain(num_send[p].at[pl.ds(1, SLOTS - 1)], num_sems.at[ITERS - 1, p, 0])
     for far, side in every:
         pair_copy(ITERS - 1, far, side).wait_send()
     for far, side in others:
         chip_copy(ITERS - 1, far, side).wait_send()
-    pltpu.make_async_copy(w_now, w_out, out_sems.at[0]).wait()
-    pltpu.make_async_copy(h_now, h_out, out_sems.at[1]).wait()
 
 
 def solution(mesh):
@@ -529,28 +534,30 @@
         groups = frames // GROUP
         block = pixels // FRAME
         hbm = pl.BlockSpec(memory_space=pl.ANY)
+        vmem = pl.BlockSpec(memory_space=pltpu.VMEM)
         dma = pltpu.SemaphoreType.DMA
         return pl.pallas_call(
             functools.partial(kernel, n_scan),
             out_shape=(
-                jax.ShapeDtypeStruct(factor_w.shape, F32),
-                jax.ShapeDtypeStruct(factor_h.shape, F32),
+                pltpu.VMEM(factor_w.shape, F32),
+                pltpu.VMEM(factor_h.shape, F32),
             ),
             in_specs=[hbm] * 5,
-            out_specs=(hbm, hbm),
+            out_specs=(vmem, vmem),
             scratch_shapes=[
                 pltpu.VMEM((groups, GROUP * FRAME, LANES), F32),
                 pltpu.VMEM((3, FRAME, 8, LANES), F32),
                 pltpu.VMEM((FRAME, GROUP, LANES), F32),
                 pltpu.VMEM((2, FRAME + 2, GROUP, LANES), F32),
+                pltpu.VMEM((2, block, frames, LANES), F32),
                 pltpu.VMEM((EY, EX, EZ, block, frames, LANES), DATA),
                 pltpu.VMEM((SLOTS, EX, block, frames, LANES), DATA),
-                *[pltpu.VMEM((ITERS + 1, SLOTS, n, rank), BF16) for _, n in PARTS],
+                tuple(pltpu.VMEM((ITERS + 1, SLOTS, n, rank), BF16) for _, n in PARTS),
                 pltpu.VMEM((frames, rank), F32),
                 pltpu.VMEM((FRAME, LANES), F32),
                 pltpu.VMEM((FRAME, LANES), F32),
-                *[pltpu.VMEM((SLOTS, n, rank), F32) for _, n in PARTS],
-                *[pltpu.VMEM((ITERS, SLOTS, n, rank), F32) for _, n in PARTS],
+                tuple(pltpu.VMEM((SLOTS, n, rank), F32) for _, n in PARTS),
+                tuple(pltpu.VMEM((ITERS, SLOTS, n, rank), F32) for _, n in PARTS),
                 pltpu.VMEM((ITERS, rank, EX * pixels), BF16),
                 pltpu.VMEM((comps, pixels), F32),
                 pltpu.VMEM((ITERS, SLOTS, 1, rank), F32),
@@ -563,15 +570,14 @@
                 dma((groups + 4,)),
                 dma((groups, 3)),
                 dma((groups,)),
-                dma((ITERS + 1, 2, 3)),
-                dma((ITERS, 2, 2)),
+                dma((ITERS + 1, len(PARTS), 3)),
+                dma((ITERS, len(PARTS), 2)),
                 dma((ITERS, mates // 2, 2)),
                 dma((ITERS, mates // 2, 2)),
                 dma((ITERS, 2)),
                 dma((ITERS, mates // 2, 2)),
                 dma((ITERS, mates // 2, 2)),
                 dma((ITERS, 2)),
-                dma((2,)),
             ],
             compiler_params=pltpu.CompilerParams(
                 collective_id=0, has_side_effects=True, vmem_limit_bytes=58 * 1024 * 1024

time: 98.1 us -> 95.5 us (0.973)
  local copies, waits for them, and re-layouts: 2.99 us -> 1.28 us
    unnamed x2, local copies, waits for them, and re-layouts: 2.99 us -> 1.28 us
where the time goes in v5:
time: 95.5 us; the launch traced here: 95.3 us
  Pallas kernels  93.4 us (98%)
  local copies, waits for them, and re-layouts  1.28 us (1%)
    pallas_call x1, Pallas kernels, local(): pl.pallas_call(functools.partial(kernel, n_scan), out_shape=(pltpu.VMEM(f...  93.4 us

profile of v5, /device:TPU:1, one launch (start us, length us, event | category | flops | bytes accessed | tf_op | source)
XLA Modules:
  0.0 95.3 jit_solution(906099372548889433)
XLA Ops:
  0.6 93.4 %shard_map.68 = (f32[48,256]{1,0:T(8,128)S(1)}, f32[64,512]{1,0:T(8,128)S(1)}) custom-call(f32[6144,128]{1,0:T(8,128)} %bitcast.1, f32[128,128]{1,0:T(8,128)} %gain_ref.1, f32[128,128]{1,0:T(8,128)} %couple_ref.1, f32[48,256]{1,0:T(8,128)} %w_ref.1, f32[64,512]{1,0:T(8,128)} %h_ref.1), custom_call_target="tpu_custom_call" | custom-call | tf_op jit(solution)/shard_map/pallas_call | solution.py:539
  94.1 0.6 copy.9
  94.7 0.7 copy.10

commit v6 on v5

--- a/solution.py
+++ b/solution.py
@@ -90,6 +90,10 @@
         other = (mx * n_scan + scan + j) % mates
         return other % n_scan, other // n_scan
 
+    def in_order(go):
+        for slot in sorted(range(1, SLOTS), key=lambda d: (min(d // EZ, EY - d // EZ) + min(d % EZ, EZ - d % EZ)), reverse=True):
+            go(slot)
+
     def remote(src, dst, sems, to_scan, y, x, z, part=0):
         return pltpu.make_async_remote_copy(
             src_ref=src,
@@ -150,19 +154,16 @@
         return pl.ds(*PARTS[p])
 
     def send_w(step, p):
-        for copy_slots in ((1, HALF), (HALF, SLOTS)):
-
-            def go(slot, carry):
-                to_slot(
-                    w_all[p].at[step, 0],
-                    w_all[p].at[step, slot],
-                    w_sems.at[step, p],
-                    ahead(slot),
-                    copy_slots[0] // HALF,
-                ).start()
-                return carry
-
-            lax.fori_loop(*copy_slots, go, 0)
+        def go(slot):
+            to_slot(
+                w_all[p].at[step, 0],
+                w_all[p].at[step, slot],
+                w_sems.at[step, p],
+                ahead(slot),
+                slot // HALF,
+            ).start()
+
+        in_order(go)
 
     def halves(u):
         _, start, count = UNITS[u]
@@ -290,7 +291,7 @@
                 return carry
 
             lax.fori_loop(0, FRAME // ROWS, sweep, 0)
-            if s == 1 and between is not None:
+            if s == 0 and between is not None:
                 between()
 
     def own_copy(g):
@@ -305,20 +306,17 @@
         own_copy(g).start()
         frames = pl.ds(g * GROUP, GROUP)
 
-        for half, (start, stop) in enumerate(((1, HALF), (HALF, SLOTS))):
-
-            def go(slot, carry):
-                y, z = ahead(slot)
-                to_slot(
-                    charge.at[y, :, z, :, frames],
-                    tile.at[slot, :, :, frames],
-                    data_sems.at[g],
-                    (y, z),
-                    half,
-                ).start()
-                return carry
-
-            lax.fori_loop(start, stop, go, 0)
+        def go(slot):
+            y, z = ahead(slot)
+            to_slot(
+                charge.at[y, :, z, :, frames],
+                tile.at[slot, :, :, frames],
+                data_sems.at[g],
+                (y, z),
+                slot // HALF,
+            ).start()
+
+        in_order(go)
 
     wide = EX * pixels
     unit_rows = [count * PARTS[p][1] for p, _, count in UNITS]
@@ -395,16 +393,15 @@
                 count, PARTS[p][1], rank
             )
 
-            def go(slot, carry):
+            def go(slot):
                 to_slot(
                     num_send[p].at[slot],
                     num_recv[p].at[it, slot],
                     num_sems.at[it, p],
                     behind(slot),
                 ).start()
-                return carry
-
-            lax.fori_loop(max(start, 1), start + count, go, 0)
+
+            in_order(go)
             if u == 0:
                 hsum_all[it, 0] = terms[unit_rows[u] : unit_rows[u] + 1]
 

time: 95.5 us -> 92.4 us (0.968)
  Pallas kernels: 93.4 us -> 90.4 us
    pallas_call x1, Pallas kernels: 93.4 us -> 90.4 us  [local(): pl.pallas_call(functools.partial(kernel, n_scan), out_shape=(pltpu.VMEM(f...]
where the time goes in v6:
time: 92.4 us; the launch traced here: 92.3 us
  Pallas kernels  90.4 us (98%)
  local copies, waits for them, and re-layouts  1.28 us (1%)
    pallas_call x1, Pallas kernels, local(): pl.pallas_call(functools.partial(kernel, n_scan), out_shape=(pltpu.VMEM(f...  90.4 us

profile of v6, /device:TPU:1, one launch (start us, length us, event | category | flops | bytes accessed | tf_op | source)
XLA Modules:
  0.0 92.3 jit_solution(2644454827314412976)
XLA Ops:
  0.6 90.4 %shard_map.68 = (f32[48,256]{1,0:T(8,128)S(1)}, f32[64,512]{1,0:T(8,128)S(1)}) custom-call(f32[6144,128]{1,0:T(8,128)} %bitcast.1, f32[128,128]{1,0:T(8,128)} %gain_ref.1, f32[128,128]{1,0:T(8,128)} %couple_ref.1, f32[48,256]{1,0:T(8,128)} %w_ref.1, f32[64,512]{1,0:T(8,128)} %h_ref.1), custom_call_target="tpu_custom_call" | custom-call | tf_op jit(solution)/shard_map/pallas_call | solution.py:536
  91.0 0.6 copy.9
  91.7 0.7 copy.10

commit v7 on v6

--- a/solution.py
+++ b/solution.py
@@ -423,7 +423,7 @@
             def add(slot, total):
                 return total + num_recv[p][it, slot]
 
-            total = lax.fori_loop(1, SLOTS, add, num_send[p][0])
+            total = lax.fori_loop(1, SLOTS, add, num_send[p][0], unroll=True)
             w_new = w_now[part_rows(p), :] * total / h_sum
             w_now[part_rows(p), :] = w_new
             w_all[p][it + 1, 0] = w_new.astype(BF16)

time: 92.4 us -> 92.3 us (level)
  no operation moved by 1% of the time
where the time goes in v7:
time: 92.3 us; the launch traced here: 92.2 us
  Pallas kernels  90.2 us (98%)
  local copies, waits for them, and re-layouts  1.28 us (1%)
    pallas_call x1, Pallas kernels, local(): pl.pallas_call(functools.partial(kernel, n_scan), out_shape=(pltpu.VMEM(f...  90.2 us

profile of v7, /device:TPU:1, one launch (start us, length us, event | category | flops | bytes accessed | tf_op | source)
XLA Modules:
  0.0 92.2 jit_solution(15119410877652387678)
XLA Ops:
  0.6 90.2 %shard_map.68 = (f32[48,256]{1,0:T(8,128)S(1)}, f32[64,512]{1,0:T(8,128)S(1)}) custom-call(f32[6144,128]{1,0:T(8,128)} %bitcast.1, f32[128,128]{1,0:T(8,128)} %gain_ref.1, f32[128,128]{1,0:T(8,128)} %couple_ref.1, f32[48,256]{1,0:T(8,128)} %w_ref.1, f32[64,512]{1,0:T(8,128)} %h_ref.1), custom_call_target="tpu_custom_call" | custom-call | tf_op jit(solution)/shard_map/pallas_call | solution.py:536
  90.9 0.6 copy.9
  91.5 0.7 copy.10
